TPU v7x, 128 devices: a whole 4x4x4 slice. The times are simulated.
128 devices in a mesh: seg: 16 (over z, y), dev: 8 (over x, core).
Axes of the slice: x: 4, y: 4, z: 4, core: 2. Of those that a mesh axis runs over, the one named last changes fastest.
Arguments:
- queries: bfloat16 [16384, 4096], P(('seg', 'dev')), may hold values from -10 to 10
- keys: bfloat16 [16384, 1024], P(('seg', 'dev')), may hold values from -10 to 10
- values: bfloat16 [16384, 1024], P(('seg', 'dev')), may hold values from -6 to 6
- doc_start: int32 [16384], P(('seg', 'dev')), may hold values from 0 to 15872, as said below
Outputs:
- attended: bfloat16 [16384, 4096], P(('seg', 'dev'))
- log_totals: float32 [32, 16384], P(None, ('seg', 'dev'))
Inputs may be any that keep to these rules, and one draw needn't show every extreme that they name: doc_start is non-decreasing, doc_start[i] <= i and i - doc_start[i] < 512; doc_start[i] = i where a document begins. The last document is the last 512 tokens; the one before it has 1 to 512 tokens; every earlier document has 128 to 512 tokens.
All inputs are finite; a program needn't handle non-finite values.
Results may differ from a plain program's by a relative error of at most 0.004.
Values may be sent and summed in bfloat16 or wider, within the bound.
No kernel may reach another device: no remote copies, remote signals or barrier semaphores. Data moves between devices by JAX's collectives and lax.ppermute only.
A program may use at most 64 MiB of HBM per device.

v0:
```python
import functools
import math

import jax
import jax.numpy as jnp
from jax import lax
from jax.experimental import pallas as pl
from jax.experimental.pallas import tpu as pltpu
from jax.sharding import PartitionSpec as P

HEAD_DIM = 128
BACK = 4
LOWEST = -1e30
SCALE = 1.0 / math.sqrt(HEAD_DIM)
LOG2E = math.log2(math.e)
AXES = ("seg", "dev")


def attend_kernel(
    pairs, group, first_ref, doc_ref, q_ref, own_k, own_v, k1, k2, k3, k4, v1, v2, v3, v4,
    out_ref, log_ref, bias_ref,
):
    rows = q_ref.shape[0]
    row = lax.broadcasted_iota(jnp.int32, (rows, rows), 0)
    col = lax.broadcasted_iota(jnp.int32, (rows, rows), 1)
    causal = col <= row

    @pl.when(pl.program_id(0) == 0)
    def _():
        start = jnp.transpose(jnp.broadcast_to(doc_ref[...], (rows, rows))) - first_ref[0]
        place = jnp.where(causal, col, col - BACK * rows)
        bias_ref[0] = jnp.where(place >= start, 0.0, LOWEST)
        for back in range(1, BACK):
            bias_ref[back] = jnp.where(col - back * rows >= start, 0.0, LOWEST)

    lane = lax.broadcasted_iota(jnp.int32, (rows, HEAD_DIM), 1)
    logs = jnp.zeros((rows, HEAD_DIM), jnp.float32)
    for pair in range(pairs):
        lo = pair * HEAD_DIM
        at = slice(lo, lo + HEAD_DIM)
        key = jnp.concatenate([own_k[:, at], k4[:, at], k1[:, at], k2[:, at], k3[:, at]], axis=0)
        value = jnp.concatenate([own_v[:, at], v4[:, at], v1[:, at], v2[:, at], v3[:, at]], axis=0)
        for head in range(group):
            wide = (pair * group + head) * HEAD_DIM
            query = q_ref[:, wide : wide + HEAD_DIM]
            raw = lax.dot_general(
                query, key, (((1,), (1,)), ((), ())), preferred_element_type=jnp.float32
            )
            near = jnp.where(causal, raw[:, :rows], raw[:, rows : 2 * rows]) + bias_ref[0]
            tiles = [near] + [
                raw[:, (back + 1) * rows : (back + 2) * rows] + bias_ref[back]
                for back in range(1, BACK)
            ]
            top = jnp.max(functools.reduce(jnp.maximum, tiles), axis=1, keepdims=True)
            expos = [jnp.exp2((tile - top) * (SCALE * LOG2E)) for tile in tiles]
            total = jnp.sum(functools.reduce(jnp.add, expos), axis=1, keepdims=True)
            rounded = [e.astype(jnp.bfloat16) for e in expos]
            zero = jnp.zeros_like(rounded[0])
            weights = jnp.concatenate(
                [jnp.where(causal, rounded[0], zero), jnp.where(causal, zero, rounded[0])]
                + rounded[1:],
                axis=1,
            )
            summed = jnp.dot(weights, value, preferred_element_type=jnp.float32)
            out_ref[:, wide : wide + HEAD_DIM] = (summed * (1.0 / total)).astype(out_ref.dtype)
            log_total = top * SCALE + jnp.log(total)
            logs = jnp.where(lane == pair * group + head, log_total, logs)
    log_ref[...] = jnp.transpose(logs)[: pairs * group]


def attention(queries, own, blocks, doc_start, first_row):
    rows, width = queries.shape
    kv_heads = own[0].shape[1] // HEAD_DIM
    group = width // own[0].shape[1]
    pairs = 2
    steps = kv_heads // pairs
    narrow = pl.BlockSpec((rows, pairs * HEAD_DIM), lambda i: (0, i))
    wide = pl.BlockSpec((rows, pairs * group * HEAD_DIM), lambda i: (0, i))
    keys = [own[0], own[1]] + [b[0] for b in blocks] + [b[1] for b in blocks]
    return pl.pallas_call(
        functools.partial(attend_kernel, pairs, group),
        grid=(steps,),
        in_specs=[
            pl.BlockSpec(memory_space=pltpu.SMEM),
            pl.BlockSpec((1, rows), lambda i: (0, 0)),
            wide,
        ]
        + [narrow] * len(keys),
        out_specs=[wide, pl.BlockSpec((pairs * group, rows), lambda i: (i, 0))],
        out_shape=[
            jax.ShapeDtypeStruct((rows, width), jnp.bfloat16),
            jax.ShapeDtypeStruct((kv_heads * group, rows), jnp.float32),
        ],
        scratch_shapes=[pltpu.VMEM((BACK, rows, rows), jnp.float32)],
        name="attend",
    )(first_row, doc_start.reshape(1, rows), queries, *keys)


def local(queries, keys, values, doc_start):
    rows = queries.shape[0]
    devices = lax.axis_size(AXES)
    me = lax.axis_index(AXES)
    first_row = (me * rows).astype(jnp.int32).reshape(1)
    odd = (me % 2) == 1

    def shifted(x, by):
        return lax.ppermute(x, AXES, [(i, i + by) for i in range(devices) if i + by < devices])

    def swapped(x):
        return lax.ppermute(x, AXES, [(i, i ^ 1) for i in range(devices)])

    two = (shifted(keys, 2), shifted(values, 2))
    four = (shifted(keys, 4), shifted(values, 4))
    near = (swapped(keys), swapped(values))
    two_swap = (swapped(two[0]), swapped(two[1]))
    four_swap = (swapped(four[0]), swapped(four[1]))
    one = tuple(jnp.where(odd, a, b) for a, b in zip(near, two_swap))
    three = tuple(jnp.where(odd, a, b) for a, b in zip(two_swap, four_swap))
    blocks = [one, two, three, four]
    return tuple(attention(queries, (keys, values), blocks, doc_start, first_row))


def solution(mesh):
    placed = (P(AXES, None), P(AXES, None), P(AXES, None), P(AXES))
    return jax.shard_map(
        local,
        mesh=mesh,
        in_specs=placed,
        out_specs=(P(AXES, None), P(None, AXES)),
        check_vma=False,
    )
```

profile of v0, /device:TPU:97, one launch (start us, length us, event | category | flops | bytes accessed | tf_op | source)
XLA Modules:
  0.0 47.2 jit_solution(2489139664441549828)
XLA Ops:
  0.6 3.1 %collective-permute-start.1 = (bf16[128,1024]{1,0:T(8,128)(2,1)}, bf16[128,1024]{1,0:T(8,128)(2,1)S(1)}, u32[]{:S(2)}, u32[]{:S(2)}) collective-permute-start(bf16[128,1024]{1,0:T(8,128)(2,1)} %own_k.1), channel_id=1, source_target_pairs={{0,2},{1,3},{2,4},{3,5},{4,6},{5,7},{6,8},{7,9},{8,10},{9,11},{10,... | collective-permute-start | bytes 786440 | tf_op jit(solution)/shard_map/ppermute | solution.py:107
  3.8 4.4 %collective-permute-start.3 = (bf16[128,1024]{1,0:T(8,128)(2,1)}, bf16[128,1024]{1,0:T(8,128)(2,1)S(1)}, u32[]{:S(2)}, u32[]{:S(2)}) collective-permute-start(bf16[128,1024]{1,0:T(8,128)(2,1)} %own_k.1), channel_id=1, source_target_pairs={{0,4},{1,5},{2,6},{3,7},{4,8},{5,9},{6,10},{7,11},{8,12},{9,13},{1... | collective-permute-start | bytes 786440 | tf_op jit(solution)/shard_map/ppermute | solution.py:107
  8.1 1.3 %collective-permute-start = (bf16[128,1024]{1,0:T(8,128)(2,1)}, bf16[128,1024]{1,0:T(8,128)(2,1)S(1)}, u32[]{:S(2)}, u32[]{:S(2)}) collective-permute-start(bf16[128,1024]{1,0:T(8,128)(2,1)} %own_k.1), channel_id=1, source_target_pairs={{0,1},{1,0},{2,3},{3,2},{4,5},{5,4},{6,7},{7,6},{8,9},{9,8},{10,11... | collective-permute-start | bytes 786440 | tf_op jit(solution)/shard_map/ppermute | solution.py:110
  9.4 2.5 %collective-permute-start.6 = (bf16[128,1024]{1,0:T(8,128)(2,1)}, bf16[128,1024]{1,0:T(8,128)(2,1)S(1)}, u32[]{:S(2)}, u32[]{:S(2)}) collective-permute-start(bf16[128,1024]{1,0:T(8,128)(2,1)} %own_v.1), channel_id=1, source_target_pairs={{0,2},{1,3},{2,4},{3,5},{4,6},{5,7},{6,8},{7,9},{8,10},{9,11},{10,... | collective-permute-start | bytes 786440 | tf_op jit(solution)/shard_map/ppermute | solution.py:107
  12.0 4.7 %collective-permute-start.8 = (bf16[128,1024]{1,0:T(8,128)(2,1)}, bf16[128,1024]{1,0:T(8,128)(2,1)S(1)}, u32[]{:S(2)}, u32[]{:S(2)}) collective-permute-start(bf16[128,1024]{1,0:T(8,128)(2,1)} %own_v.1), channel_id=1, source_target_pairs={{0,4},{1,5},{2,6},{3,7},{4,8},{5,9},{6,10},{7,11},{8,12},{9,13},{1... | collective-permute-start | bytes 786440 | tf_op jit(solution)/shard_map/ppermute | solution.py:107
  16.6 0.0 collective-permute-done.1.k2
  16.6 0.0 copy-start
  16.6 0.7 %collective-permute-start.2 = (bf16[128,1024]{1,0:T(8,128)(2,1)S(1)}, bf16[128,1024]{1,0:T(8,128)(2,1)S(1)}, u32[]{:S(2)}, u32[]{:S(2)}) collective-permute-start(bf16[128,1024]{1,0:T(8,128)(2,1)S(1)} %collective-permute-done.1.k2), channel_id=1, source_target_pairs={{0,1},{1,0},{2,3},{3,2},{4,5},{5,4},{6,7},{7,6},{8,9},{9,8},{10,11... | collective-permute-start | bytes 786440 | tf_op jit(solution)/shard_map/ppermute | solution.py:110
  17.3 2.7 %collective-permute-done.3.k4 = bf16[128,1024]{1,0:T(8,128)(2,1)S(1)} collective-permute-done((bf16[128,1024]{1,0:T(8,128)(2,1)}, bf16[128,1024]{1,0:T(8,128)(2,1)S(1)}, u32[]{:S(2)}, u32[]{:S(2)}) %collective-permute-start.3) | collective-permute-done | bytes 262176 | tf_op jit(solution)/shard_map/ppermute | solution.py:107
  20.0 0.0 copy-start.1
  20.0 2.7 %collective-permute-start.4 = (bf16[128,1024]{1,0:T(8,128)(2,1)S(1)}, bf16[128,1024]{1,0:T(8,128)(2,1)S(1)}, u32[]{:S(2)}, u32[]{:S(2)}) collective-permute-start(bf16[128,1024]{1,0:T(8,128)(2,1)S(1)} %collective-permute-done.3.k4), channel_id=1, source_target_pairs={{0,1},{1,0},{2,3},{3,2},{4,5},{5,4},{6,7},{7,6},{8,9},{9,8},{10,11... | collective-permute-start | bytes 786440 | tf_op jit(solution)/shard_map/ppermute | solution.py:110
  22.7 0.0 collective-permute-done
  22.7 0.1 collective-permute-start.5
  22.8 5.0 %collective-permute-done.6.v2 = bf16[128,1024]{1,0:T(8,128)(2,1)S(1)} collective-permute-done((bf16[128,1024]{1,0:T(8,128)(2,1)}, bf16[128,1024]{1,0:T(8,128)(2,1)S(1)}, u32[]{:S(2)}, u32[]{:S(2)}) %collective-permute-start.6) | collective-permute-done | bytes 262176 | tf_op jit(solution)/shard_map/ppermute | solution.py:107
  27.8 0.0 copy-start.2
  27.8 0.5 %collective-permute-start.7 = (bf16[128,1024]{1,0:T(8,128)(2,1)S(1)}, bf16[128,1024]{1,0:T(8,128)(2,1)S(1)}, u32[]{:S(2)}, u32[]{:S(2)}) collective-permute-start(bf16[128,1024]{1,0:T(8,128)(2,1)S(1)} %collective-permute-done.6.v2), channel_id=1, source_target_pairs={{0,1},{1,0},{2,3},{3,2},{4,5},{5,4},{6,7},{7,6},{8,9},{9,8},{10,11... | collective-permute-start | bytes 786440 | tf_op jit(solution)/shard_map/ppermute | solution.py:110
  28.3 2.9 %collective-permute-done.8.v4 = bf16[128,1024]{1,0:T(8,128)(2,1)S(1)} collective-permute-done((bf16[128,1024]{1,0:T(8,128)(2,1)}, bf16[128,1024]{1,0:T(8,128)(2,1)S(1)}, u32[]{:S(2)}, u32[]{:S(2)}) %collective-permute-start.8) | collective-permute-done | bytes 262176 | tf_op jit(solution)/shard_map/ppermute | solution.py:107
  31.3 0.0 copy-start.3
  31.3 1.5 %collective-permute-start.9 = (bf16[128,1024]{1,0:T(8,128)(2,1)S(1)}, bf16[128,1024]{1,0:T(8,128)(2,1)S(1)}, u32[]{:S(2)}, u32[]{:S(2)}) collective-permute-start(bf16[128,1024]{1,0:T(8,128)(2,1)S(1)} %collective-permute-done.8.v4), channel_id=1, source_target_pairs={{0,1},{1,0},{2,3},{3,2},{4,5},{5,4},{6,7},{7,6},{8,9},{9,8},{10,11... | collective-permute-start | bytes 786440 | tf_op jit(solution)/shard_map/ppermute | solution.py:110
  32.8 0.0 collective-permute-done.2
  32.8 0.0 collective-permute-done.4
  32.8 0.8 %broadcast_select_fusion.2 = (bf16[128,1024]{1,0:T(8,128)(2,1)}, bf16[128,1024]{1,0:T(8,128)(2,1)}) fusion(bf16[128,1024]{1,0:T(8,128)(2,1)S(1)} %collective-permute-done.2, bf16[128,1024]{1,0:T(8,128)(2,1)S(1)} %collective-permute-done.4, pred[]{:T(512)S(6)} %eq.5, bf16[128,1024]{1,0:T(8,128)(2,1)S(1)} %collective-permute-done), kind=kLoop, calls=%fused_computation.2 | loop fusion | flops 262144 | bytes 1310721 | tf_op jit(solution)/shard_map/jit(_where)/select_n | solution.py:118
  33.6 0.0 copy-done
  33.6 0.0 copy-done.1
  33.6 0.0 copy-done.2
  33.7 0.0 copy-done.3
  33.7 0.0 collective-permute-done.5
  33.7 0.0 collective-permute-done.7
  33.7 0.3 collective-permute-done.9
  34.0 0.9 %broadcast_select_fusion = (bf16[128,1024]{1,0:T(8,128)(2,1)}, bf16[128,1024]{1,0:T(8,128)(2,1)}) fusion(bf16[128,1024]{1,0:T(8,128)(2,1)S(1)} %collective-permute-done.7, bf16[128,1024]{1,0:T(8,128)(2,1)S(1)} %collective-permute-done.9, pred[]{:T(512)S(6)} %eq.5, bf16[128,1024]{1,0:T(8,128)(2,1)S(1)} %collective-permute-done.5), kind=kLoop, calls=%fused_computation | loop fusion | flops 262144 | bytes 1310721 | tf_op jit(solution)/shard_map/jit(_where)/select_n | solution.py:118
  34.8 12.4 %attend.1 = (bf16[128,4096]{1,0:T(8,128)(2,1)}, f32[32,128]{1,0:T(8,128)}) custom-call(s32[1]{0:T(128)} %bitcast.first_ref, s32[1,128]{1,0:T(1,128)} %bitcast.2, bf16[128,4096]{1,0:T(8,128)(2,1)} %q_ref.1, bf16[128,1024]{1,0:T(8,128)(2,1)} %own_k.1, bf16[128,1024]{1,0:T(8,128)(2,1)} %own_v.1, bf16[128,1024]{1,0:T(8,128)(2,1)} %get-tuple-element.5.k1, ...), custom_call_target="tpu_custom_call" | custom-call | tf_op jit(solution)/shard_map/attend/pallas_call | solution.py:80
Async XLA Ops:
  0.6 16.0 %collective-permute-start.1 = (bf16[128,1024]{1,0:T(8,128)(2,1)}, bf16[128,1024]{1,0:T(8,128)(2,1)S(1)}, u32[]{:S(2)}, u32[]{:S(2)}) collective-permute-start(bf16[128,1024]{1,0:T(8,128)(2,1)} %own_k.1), channel_id=1, source_target_pairs={{0,2},{1,3},{2,4},{3,5},{4,6},{5,7},{6,8},{7,9},{8,10},{9,11},{10,... | collective-permute-start | bytes 786440 | tf_op jit(solution)/shard_map/ppermute | solution.py:107
  3.8 16.3 %collective-permute-start.3 = (bf16[128,1024]{1,0:T(8,128)(2,1)}, bf16[128,1024]{1,0:T(8,128)(2,1)S(1)}, u32[]{:S(2)}, u32[]{:S(2)}) collective-permute-start(bf16[128,1024]{1,0:T(8,128)(2,1)} %own_k.1), channel_id=1, source_target_pairs={{0,4},{1,5},{2,6},{3,7},{4,8},{5,9},{6,10},{7,11},{8,12},{9,13},{1... | collective-permute-start | bytes 786440 | tf_op jit(solution)/shard_map/ppermute | solution.py:107
  8.1 14.6 %collective-permute-start = (bf16[128,1024]{1,0:T(8,128)(2,1)}, bf16[128,1024]{1,0:T(8,128)(2,1)S(1)}, u32[]{:S(2)}, u32[]{:S(2)}) collective-permute-start(bf16[128,1024]{1,0:T(8,128)(2,1)} %own_k.1), channel_id=1, source_target_pairs={{0,1},{1,0},{2,3},{3,2},{4,5},{5,4},{6,7},{7,6},{8,9},{9,8},{10,11... | collective-permute-start | bytes 786440 | tf_op jit(solution)/shard_map/ppermute | solution.py:110
  9.4 18.4 %collective-permute-start.6 = (bf16[128,1024]{1,0:T(8,128)(2,1)}, bf16[128,1024]{1,0:T(8,128)(2,1)S(1)}, u32[]{:S(2)}, u32[]{:S(2)}) collective-permute-start(bf16[128,1024]{1,0:T(8,128)(2,1)} %own_v.1), channel_id=1, source_target_pairs={{0,2},{1,3},{2,4},{3,5},{4,6},{5,7},{6,8},{7,9},{8,10},{9,11},{10,... | collective-permute-start | bytes 786440 | tf_op jit(solution)/shard_map/ppermute | solution.py:107
  12.0 19.3 %collective-permute-start.8 = (bf16[128,1024]{1,0:T(8,128)(2,1)}, bf16[128,1024]{1,0:T(8,128)(2,1)S(1)}, u32[]{:S(2)}, u32[]{:S(2)}) collective-permute-start(bf16[128,1024]{1,0:T(8,128)(2,1)} %own_v.1), channel_id=1, source_target_pairs={{0,4},{1,5},{2,6},{3,7},{4,8},{5,9},{6,10},{7,11},{8,12},{9,13},{1... | collective-permute-start | bytes 786440 | tf_op jit(solution)/shard_map/ppermute | solution.py:107
  16.6 17.0 %copy-start = (bf16[128,1024]{1,0:T(8,128)(2,1)}, bf16[128,1024]{1,0:T(8,128)(2,1)S(1)}, u32[]{:S(2)}) copy-start(bf16[128,1024]{1,0:T(8,128)(2,1)S(1)} %collective-permute-done.1.k2) | copy-start | bytes 786436
  16.6 16.2 %collective-permute-start.2 = (bf16[128,1024]{1,0:T(8,128)(2,1)S(1)}, bf16[128,1024]{1,0:T(8,128)(2,1)S(1)}, u32[]{:S(2)}, u32[]{:S(2)}) collective-permute-start(bf16[128,1024]{1,0:T(8,128)(2,1)S(1)} %collective-permute-done.1.k2), channel_id=1, source_target_pairs={{0,1},{1,0},{2,3},{3,2},{4,5},{5,4},{6,7},{7,6},{8,9},{9,8},{10,11... | collective-permute-start | bytes 786440 | tf_op jit(solution)/shard_map/ppermute | solution.py:110
  20.0 13.6 %copy-start.1 = (bf16[128,1024]{1,0:T(8,128)(2,1)}, bf16[128,1024]{1,0:T(8,128)(2,1)S(1)}, u32[]{:S(2)}) copy-start(bf16[128,1024]{1,0:T(8,128)(2,1)S(1)} %collective-permute-done.3.k4) | copy-start | bytes 786436
  20.0 12.8 %collective-permute-start.4 = (bf16[128,1024]{1,0:T(8,128)(2,1)S(1)}, bf16[128,1024]{1,0:T(8,128)(2,1)S(1)}, u32[]{:S(2)}, u32[]{:S(2)}) collective-permute-start(bf16[128,1024]{1,0:T(8,128)(2,1)S(1)} %collective-permute-done.3.k4), channel_id=1, source_target_pairs={{0,1},{1,0},{2,3},{3,2},{4,5},{5,4},{6,7},{7,6},{8,9},{9,8},{10,11... | collective-permute-start | bytes 786440 | tf_op jit(solution)/shard_map/ppermute | solution.py:110
  22.7 11.0 %collective-permute-start.5 = (bf16[128,1024]{1,0:T(8,128)(2,1)}, bf16[128,1024]{1,0:T(8,128)(2,1)S(1)}, u32[]{:S(2)}, u32[]{:S(2)}) collective-permute-start(bf16[128,1024]{1,0:T(8,128)(2,1)} %own_v.1), channel_id=1, source_target_pairs={{0,1},{1,0},{2,3},{3,2},{4,5},{5,4},{6,7},{7,6},{8,9},{9,8},{10,11... | collective-permute-start | bytes 786440 | tf_op jit(solution)/shard_map/ppermute | solution.py:110
  27.8 5.8 %copy-start.2 = (bf16[128,1024]{1,0:T(8,128)(2,1)}, bf16[128,1024]{1,0:T(8,128)(2,1)S(1)}, u32[]{:S(2)}) copy-start(bf16[128,1024]{1,0:T(8,128)(2,1)S(1)} %collective-permute-done.6.v2) | copy-start | bytes 786436
  27.8 5.8 %collective-permute-start.7 = (bf16[128,1024]{1,0:T(8,128)(2,1)S(1)}, bf16[128,1024]{1,0:T(8,128)(2,1)S(1)}, u32[]{:S(2)}, u32[]{:S(2)}) collective-permute-start(bf16[128,1024]{1,0:T(8,128)(2,1)S(1)} %collective-permute-done.6.v2), channel_id=1, source_target_pairs={{0,1},{1,0},{2,3},{3,2},{4,5},{5,4},{6,7},{7,6},{8,9},{9,8},{10,11... | collective-permute-start | bytes 786440 | tf_op jit(solution)/shard_map/ppermute | solution.py:110
  31.3 2.4 %copy-start.3 = (bf16[128,1024]{1,0:T(8,128)(2,1)}, bf16[128,1024]{1,0:T(8,128)(2,1)S(1)}, u32[]{:S(2)}) copy-start(bf16[128,1024]{1,0:T(8,128)(2,1)S(1)} %collective-permute-done.8.v4) | copy-start | bytes 786436
  31.3 2.7 %collective-permute-start.9 = (bf16[128,1024]{1,0:T(8,128)(2,1)S(1)}, bf16[128,1024]{1,0:T(8,128)(2,1)S(1)}, u32[]{:S(2)}, u32[]{:S(2)}) collective-permute-start(bf16[128,1024]{1,0:T(8,128)(2,1)S(1)} %collective-permute-done.8.v4), channel_id=1, source_target_pairs={{0,1},{1,0},{2,3},{3,2},{4,5},{5,4},{6,7},{7,6},{8,9},{9,8},{10,11... | collective-permute-start | bytes 786440 | tf_op jit(solution)/shard_map/ppermute | solution.py:110
where the time goes:
time: 47.4 us; the launch traced here: 47.2 us
  starting transfers between devices  21.4 us (45%)
  Pallas kernels  12.4 us (26%)
  waiting for transfers between devices  11 us (23%)
  other arithmetic  1.71 us (4%)
  between operations  0.71 us (1%)
    ppermute x4, starting transfers between devices, shifted(): lax.ppermute(x, AXES, [(i, i + by) for i in range(devices) if i + by < de...  14.6 us
    pallas_call x1, Pallas kernels, attention(): pl.pallas_call(functools.partial(attend_kernel, pairs, group), grid=(step...  12.4 us
    ppermute x4, waiting for transfers between devices, shifted(): lax.ppermute(x, AXES, [(i, i + by) for i in range(devices) if i + by < de...  10.7 us
    ppermute x6, starting transfers between devices, swapped(): return lax.ppermute(x, AXES, [(i, i ^ 1) for i in range(devices)])  6.79 us
    select_n x2, other arithmetic, local(): three = tuple((jnp.where(odd, a, b) for a, b in zip(two_swap, four_swap)))  1.71 us
  transfers between devices with their start and end apart: 10, of which 4 were waited for; matrix products, arithmetic and copies ran while one was open for 2% of the time, Pallas kernels for 0%

commit v1 on v0

v1 whole, which is shorter than its diff:
```python
import functools
import math

import jax
import jax.numpy as jnp
from jax import lax
from jax.experimental import pallas as pl
from jax.experimental.pallas import tpu as pltpu
from jax.sharding import PartitionSpec as P

HEAD_DIM = 128
BACK = 4
LOWEST = -1e30
SCALE = 1.0 / math.sqrt(HEAD_DIM)
LOG2E = math.log2(math.e)
AXES = ("seg", "dev")


def causal_tile(rows):
    key = lax.broadcasted_iota(jnp.int32, (rows, rows), 0)
    query = lax.broadcasted_iota(jnp.int32, (rows, rows), 1)
    return key <= query, key


def in_order(here_ref, blocks, at):
    own, near, two, two_swap, four, four_swap = (b[:, at] for b in blocks)
    odd = jnp.full(own.shape, here_ref[1], jnp.int32) == 1
    one = jnp.where(odd, near, two_swap)
    three = jnp.where(odd, two_swap, four_swap)
    return jnp.concatenate([own, four, one, two, three], axis=0)


def scores_kernel(pairs, group, here_ref, doc_ref, q_ref, *refs):
    blocks, (weight_ref, inverse_ref, log_ref, bias_ref) = refs[:6], refs[6:]
    rows = q_ref.shape[0]
    causal, place = causal_tile(rows)

    start = jnp.broadcast_to(doc_ref[...] - here_ref[0], (rows, rows))
    merged = jnp.where(causal, place, place - BACK * rows)
    bias_ref[0] = jnp.where(merged >= start, 0.0, LOWEST)
    for back in range(1, BACK):
        bias_ref[back] = jnp.where(place - back * rows >= start, 0.0, LOWEST)

    for pair in range(pairs):
        key = in_order(here_ref, blocks, slice(pair * HEAD_DIM, (pair + 1) * HEAD_DIM))
        for g in range(group):
            head = pair * group + g
            raw = lax.dot_general(
                key,
                q_ref[:, head * HEAD_DIM : (head + 1) * HEAD_DIM],
                (((1,), (1,)), ((), ())),
                preferred_element_type=jnp.float32,
            )
            tiles = [jnp.where(causal, raw[:rows], raw[rows : 2 * rows]) + bias_ref[0]] + [
                raw[(back + 1) * rows : (back + 2) * rows] + bias_ref[back]
                for back in range(1, BACK)
            ]
            top = jnp.max(functools.reduce(jnp.maximum, tiles), axis=0, keepdims=True)
            expos = [jnp.exp2((tile - top) * (SCALE * LOG2E)) for tile in tiles]
            total = jnp.sum(functools.reduce(jnp.add, expos), axis=0, keepdims=True)
            for index, e in enumerate(expos):
                weight_ref[
                    (pair * BACK + index) * rows : (pair * BACK + index + 1) * rows,
                    g * rows : (g + 1) * rows,
                ] = e.astype(jnp.bfloat16)
            log_ref[head : head + 1] = top * SCALE + jnp.log(total)
            inverse_ref[head : head + 1] = 1.0 / total


def values_kernel(pairs, group, here_ref, weight_ref, inverse_ref, *refs):
    blocks, out_ref = refs[:6], refs[6]
    rows = out_ref.shape[0]
    causal, _ = causal_tile(rows)
    causal = jnp.concatenate([causal] * group, axis=1)
    for pair in range(pairs):
        value = in_order(here_ref, blocks, slice(pair * HEAD_DIM, (pair + 1) * HEAD_DIM))
        weights = weight_ref[pair * BACK * rows : (pair + 1) * BACK * rows]
        near = weights[:rows]
        zero = jnp.zeros_like(near)
        weights = jnp.concatenate(
            [jnp.where(causal, near, zero), jnp.where(causal, zero, near), weights[rows:]], axis=0
        )
        summed = lax.dot_general(
            value, weights, (((0,), (0,)), ((), ())), preferred_element_type=jnp.float32
        )
        for g in range(group):
            head = pair * group + g
            out_ref[:, head * HEAD_DIM : (head + 1) * HEAD_DIM] = jnp.transpose(
                (summed[:, g * rows : (g + 1) * rows] * inverse_ref[head : head + 1]).astype(
                    out_ref.dtype
                )
            )


def weigh(queries, keys, doc_start, here):
    rows, width = queries.shape
    kv_heads = keys[0].shape[1] // HEAD_DIM
    group = width // keys[0].shape[1]
    heads = kv_heads * group
    reach = BACK * rows
    whole = pl.BlockSpec(memory_space=pltpu.VMEM)
    return pl.pallas_call(
        functools.partial(scores_kernel, kv_heads, group),
        in_specs=[pl.BlockSpec(memory_space=pltpu.SMEM)] + [whole] * 8,
        out_specs=[whole] * 3,
        out_shape=[
            jax.ShapeDtypeStruct((kv_heads * reach, group * rows), jnp.bfloat16),
            jax.ShapeDtypeStruct((heads, rows), jnp.float32),
            jax.ShapeDtypeStruct((heads, rows), jnp.float32),
        ],
        scratch_shapes=[pltpu.VMEM((BACK, rows, rows), jnp.float32)],
        cost_estimate=pl.CostEstimate(
            flops=2 * rows * (reach + rows) * width,
            bytes_accessed=8 << 20,
            transcendentals=rows * reach * heads,
        ),
        compiler_params=pltpu.CompilerParams(vmem_limit_bytes=32 << 20),
        name="scores",
    )(here, doc_start.reshape(1, rows), queries, *keys)


def combine(weights, inverses, values, here, width):
    rows = values[0].shape[0]
    kv_heads = values[0].shape[1] // HEAD_DIM
    group = width // values[0].shape[1]
    whole = pl.BlockSpec(memory_space=pltpu.VMEM)
    return pl.pallas_call(
        functools.partial(values_kernel, kv_heads, group),
        in_specs=[pl.BlockSpec(memory_space=pltpu.SMEM)] + [whole] * 8,
        out_specs=whole,
        out_shape=jax.ShapeDtypeStruct((rows, width), jnp.bfloat16),
        cost_estimate=pl.CostEstimate(
            flops=2 * rows * (BACK + 1) * rows * width, bytes_accessed=8 << 20, transcendentals=0
        ),
        compiler_params=pltpu.CompilerParams(vmem_limit_bytes=32 << 20),
        name="values",
    )(here, weights, inverses, *values)


def local(queries, keys, values, doc_start):
    rows, width = queries.shape
    devices = lax.axis_size(AXES)
    me = lax.axis_index(AXES)
    here = jnp.stack([me * rows, me % 2]).astype(jnp.int32)
    chain = devices - BACK

    def two_back(x):
        pairs = [(i, (i + 2) % chain) for i in range(chain)]
        pairs += [(chain + i, chain + (i + 2) % BACK) for i in range(BACK)]
        return lax.ppermute(x, AXES, pairs)

    def four_back(x):
        return lax.ppermute(x, AXES, [(i, i + 4) for i in range(chain - 4)])

    def swapped(x):
        return lax.ppermute(x, AXES, [(i, i ^ 1) for i in range(devices)])

    key_near = swapped(keys)
    key_two, key_four = two_back(keys), four_back(keys)
    value_two, value_four = two_back(values), four_back(values)
    value_near = swapped(values)
    key_two_swap, key_four_swap = lax.cond(
        doc_start[0] >= 0,
        lambda a, b: (swapped(a), swapped(b)),
        lambda a, b: (a, b),
        key_two,
        key_four,
    )
    all_keys = (keys, key_near, key_two, key_two_swap, key_four, key_four_swap)
    weights, inverses, logs = weigh(queries, all_keys, doc_start, here)
    value_two, value_four, weights = lax.optimization_barrier((value_two, value_four, weights))
    all_values = (
        values, value_near, value_two, swapped(value_two), value_four, swapped(value_four)
    )
    return combine(weights, inverses, all_values, here, width), logs


def solution(mesh):
    placed = (P(AXES, None), P(AXES, None), P(AXES, None), P(AXES))
    return jax.shard_map(
        local,
        mesh=mesh,
        in_specs=placed,
        out_specs=(P(AXES, None), P(None, AXES)),
        check_vma=False,
    )
```

time: 47.4 us -> 36.1 us (0.76)
  starting transfers between devices: 21.4 us -> 15.4 us
  Pallas kernels: 12.4 us -> 7.9 us
  local copies, waits for them, and re-layouts: 0.02 us -> 2.84 us
  waiting for transfers between devices: 11 us -> 8.29 us
  other arithmetic: 1.71 us -> 0.07 us
  between operations: 0.71 us -> 1.33 us
    ppermute x4, waiting for transfers between devices: 10.7 us -> 5.23 us  [the longest x2 5.22 us: four_back(): return lax.ppermute(x, AXES, [(i, i + 4) for i in range(chain - 4)])]
    pallas_call x1 -> x2, Pallas kernels: 12.4 us -> 7.9 us  [the longest x1 5.16 us: weigh(): pl.pallas_call(functools.partial(scores_kernel, kv_heads, group), in_spec...]
    ppermute x4, starting transfers between devices: 14.6 us -> 10.3 us  [the longest x2 7.78 us: four_back(): return lax.ppermute(x, AXES, [(i, i + 4) for i in range(chain - 4)])]
    unnamed x8, local copies, waits for them, and re-layouts: 0.02 us -> 2.84 us
    ppermute x6, waiting for transfers between devices: 0.29 us -> 3.07 us  [swapped(): return lax.ppermute(x, AXES, [(i, i ^ 1) for i in range(devices)])]
    ppermute x6, starting transfers between devices: 6.79 us -> 5.07 us  [swapped(): return lax.ppermute(x, AXES, [(i, i ^ 1) for i in range(devices)])]
    select_n x2 -> x0, other arithmetic: 1.71 us -> none  [local(): three = tuple((jnp.where(odd, a, b) for a, b in zip(two_swap, four_swap)))]
  transfers between devices with their start and end apart: 10 -> 10, of which waited for: 4 -> 5; matrix products, arithmetic and copies ran while one was open for 2% -> 0% of each run, Pallas kernels for 0% -> 14%
where the time goes in v1:
time: 36.1 us; the launch traced here: 35.8 us
  starting transfers between devices  15.4 us (43%)
  waiting for transfers between devices  8.29 us (23%)
  Pallas kernels  7.9 us (22%)
  local copies, waits for them, and re-layouts  2.84 us (8%)
  between operations  1.33 us (4%)
    ppermute x2, starting transfers between devices, four_back(): return lax.ppermute(x, AXES, [(i, i + 4) for i in range(chain - 4)])  7.78 us
    ppermute x2, waiting for transfers between devices, four_back(): return lax.ppermute(x, AXES, [(i, i + 4) for i in range(chain - 4)])  5.22 us
    pallas_call x1, Pallas kernels, weigh(): pl.pallas_call(functools.partial(scores_kernel, kv_heads, group), in_spec...  5.16 us
    ppermute x6, starting transfers between devices, swapped(): return lax.ppermute(x, AXES, [(i, i ^ 1) for i in range(devices)])  5.07 us
    ppermute x6, waiting for transfers between devices, swapped(): return lax.ppermute(x, AXES, [(i, i ^ 1) for i in range(devices)])  3.07 us
    unnamed x8, local copies, waits for them, and re-layouts  2.84 us
    pallas_call x1, Pallas kernels, combine(): pl.pallas_call(functools.partial(values_kernel, kv_heads, group), in_spec...  2.75 us
    ppermute x2, starting transfers between devices, two_back(): return lax.ppermute(x, AXES, pairs)  2.56 us
  transfers between devices with their start and end apart: 10, of which 5 were waited for; matrix products, arithmetic and copies ran while one was open for 0% of the time, Pallas kernels for 14%

profile of v1, /device:TPU:97, one launch (start us, length us, event | category | flops | bytes accessed | tf_op | source)
XLA Modules:
  0.0 35.8 jit_solution(11212199394820858673)
XLA Ops:
  0.6 0.0 copy-start
  0.6 1.3 %collective-permute-start.5 = (bf16[128,1024]{1,0:T(8,128)(2,1)}, bf16[128,1024]{1,0:T(8,128)(2,1)S(1)}, u32[]{:S(2)}, u32[]{:S(2)}) collective-permute-start(bf16[128,1024]{1,0:T(8,128)(2,1)} %refs_0_.2), channel_id=1, source_target_pairs={{0,2},{1,3},{2,4},{3,5},{4,6},{5,7},{6,8},{7,9},{8,10},{9,11},{10,... | collective-permute-start | bytes 786440 | tf_op jit(solution)/shard_map/ppermute | solution.py:150
  1.9 4.3 %collective-permute-start.6 = (bf16[128,1024]{1,0:T(8,128)(2,1)}, bf16[128,1024]{1,0:T(8,128)(2,1)S(1)}, u32[]{:S(2)}, u32[]{:S(2)}) collective-permute-start(bf16[128,1024]{1,0:T(8,128)(2,1)} %refs_0_.2), channel_id=1, source_target_pairs={{0,4},{1,5},{2,6},{3,7},{4,8},{5,9},{6,10},{7,11},{8,12},{9,13},{1... | collective-permute-start | bytes 786440 | tf_op jit(solution)/shard_map/ppermute | solution.py:153
  6.3 1.3 %collective-permute-start.4 = (bf16[128,1024]{1,0:T(8,128)(2,1)}, bf16[128,1024]{1,0:T(8,128)(2,1)S(1)}, u32[]{:S(2)}, u32[]{:S(2)}) collective-permute-start(bf16[128,1024]{1,0:T(8,128)(2,1)} %refs_0_.2), channel_id=1, source_target_pairs={{0,1},{1,0},{2,3},{3,2},{4,5},{5,4},{6,7},{7,6},{8,9},{9,8},{10,11... | collective-permute-start | bytes 786440 | tf_op jit(solution)/shard_map/ppermute | solution.py:156
  7.6 3.4 %collective-permute-start.3 = (bf16[128,1024]{1,0:T(8,128)(2,1)}, bf16[128,1024]{1,0:T(8,128)(2,1)S(1)}, u32[]{:S(2)}, u32[]{:S(2)}) collective-permute-start(bf16[128,1024]{1,0:T(8,128)(2,1)} %refs_0_.3), channel_id=1, source_target_pairs={{0,4},{1,5},{2,6},{3,7},{4,8},{5,9},{6,10},{7,11},{8,12},{9,13},{1... | collective-permute-start | bytes 786440 | tf_op jit(solution)/shard_map/ppermute | solution.py:153
  11.0 1.3 %collective-permute-start.2 = (bf16[128,1024]{1,0:T(8,128)(2,1)}, bf16[128,1024]{1,0:T(8,128)(2,1)S(1)}, u32[]{:S(2)}, u32[]{:S(2)}) collective-permute-start(bf16[128,1024]{1,0:T(8,128)(2,1)} %refs_0_.3), channel_id=1, source_target_pairs={{0,2},{1,3},{2,4},{3,5},{4,6},{5,7},{6,8},{7,9},{8,10},{9,11},{10,... | collective-permute-start | bytes 786440 | tf_op jit(solution)/shard_map/ppermute | solution.py:150
  13.0 0.0 collective-permute-done.5.refs_2_
  13.0 5.2 %collective-permute-done.6.refs_4_ = bf16[128,1024]{1,0:T(8,128)(2,1)S(1)} collective-permute-done((bf16[128,1024]{1,0:T(8,128)(2,1)}, bf16[128,1024]{1,0:T(8,128)(2,1)S(1)}, u32[]{:S(2)}, u32[]{:S(2)}) %collective-permute-start.6) | collective-permute-done | bytes 262176 | tf_op jit(solution)/shard_map/ppermute | solution.py:153
  18.2 4.5 %conditional.1 = (bf16[128,1024]{1,0:T(8,128)(2,1)}, bf16[128,1024]{1,0:T(8,128)(2,1)}) conditional(s32[]{:T(128)} %bitcast.3, (bf16[128,1024]{1,0:T(8,128)(2,1)S(1)}, bf16[128,1024]{1,0:T(8,128)(2,1)S(1)}) %tuple.16, (bf16[128,1024]{1,0:T(8,128)(2,1)S(1)}, bf16[128,1024]{1,0:T(8,128)(2,1)S(1)}) %tuple.16), branch_computations={%region_0.1_spmd, %region_1.2_spmd} | conditional | bytes 2097248 | solution.py:162
  18.2 2.8 %collective-permute-start = (bf16[128,1024]{1,0:T(8,128)(2,1)S(1)}, bf16[128,1024]{1,0:T(8,128)(2,1)}, u32[]{:S(2)}, u32[]{:S(2)}) collective-permute-start(bf16[128,1024]{1,0:T(8,128)(2,1)S(1)} %get-tuple-element.8), channel_id=1, source_target_pairs={{0,1},{1,0},{2,3},{3,2},{4,5},{5,4},{6,7},{7,6},{8,9},{9,8},{10,11... | collective-permute-start | bytes 786440 | tf_op jit(solution)/shard_map/cond/branch_1_fun/ppermute | solution.py:156
  21.0 0.0 collective-permute-start.1
  21.0 1.3 %collective-permute-done = bf16[128,1024]{1,0:T(8,128)(2,1)} collective-permute-done((bf16[128,1024]{1,0:T(8,128)(2,1)S(1)}, bf16[128,1024]{1,0:T(8,128)(2,1)}, u32[]{:S(2)}, u32[]{:S(2)}) %collective-permute-start) | collective-permute-done | bytes 262176 | tf_op jit(solution)/shard_map/cond/branch_1_fun/ppermute | solution.py:156
  22.3 0.4 %collective-permute-done.1 = bf16[128,1024]{1,0:T(8,128)(2,1)} collective-permute-done((bf16[128,1024]{1,0:T(8,128)(2,1)S(1)}, bf16[128,1024]{1,0:T(8,128)(2,1)}, u32[]{:S(2)}, u32[]{:S(2)}) %collective-permute-start.1) | collective-permute-done | bytes 262176 | tf_op jit(solution)/shard_map/cond/branch_1_fun/ppermute | solution.py:156
  22.7 0.4 %collective-permute-start.7 = (bf16[128,1024]{1,0:T(8,128)(2,1)}, bf16[128,1024]{1,0:T(8,128)(2,1)S(1)}, u32[]{:S(2)}, u32[]{:S(2)}) collective-permute-start(bf16[128,1024]{1,0:T(8,128)(2,1)} %refs_0_.3), channel_id=1, source_target_pairs={{0,1},{1,0},{2,3},{3,2},{4,5},{5,4},{6,7},{7,6},{8,9},{9,8},{10,11... | collective-permute-start | bytes 786440 | tf_op jit(solution)/shard_map/ppermute | solution.py:156
  23.0 0.1 pad_add_fusion.here_ref
  23.1 0.0 collective-permute-done.4.refs_1_
  23.1 0.0 copy-start.1
  23.1 1.2 %copy-done.1 = bf16[128,4096]{1,0:T(8,128)(2,1)S(1)} copy-done((bf16[128,4096]{1,0:T(8,128)(2,1)S(1)}, bf16[128,4096]{1,0:T(8,128)(2,1)}, u32[]{:S(2)}) %copy-start.1) | copy-done | bytes 1048600
  24.3 0.0 copy-start.2
  24.3 0.9 %copy-done.2 = bf16[128,1024]{1,0:T(8,128)(2,1)S(1)} copy-done((bf16[128,1024]{1,0:T(8,128)(2,1)S(1)}, bf16[128,1024]{1,0:T(8,128)(2,1)}, u32[]{:S(2)}) %copy-start.2) | copy-done | bytes 262168
  25.3 0.0 copy-start.3
  25.3 0.7 %copy-done.3 = s32[128]{0:T(128)S(1)} copy-done((s32[128]{0:T(128)S(1)}, s32[128]{0:T(128)}, u32[]{:S(2)}) %copy-start.3) | copy-done | bytes 536
  25.9 5.2 %scores.1 = (bf16[4096,512]{1,0:T(8,128)(2,1)S(1)}, f32[32,128]{1,0:T(8,128)S(1)}, f32[32,128]{1,0:T(8,128)}) custom-call(s32[2]{0:T(128)S(1)} %pad_add_fusion.here_ref, s32[1,128]{1,0:T(1,128)S(1)} %bitcast.6, bf16[128,4096]{1,0:T(8,128)(2,1)S(1)} %copy-done.1, bf16[128,1024]{1,0:T(8,128)(2,1)S(1)} %copy-done.2, ...), custom_call_target="tpu_custom_call" | custom-call | flops 671088640 | bytes 8388608 | tf_op jit(solution)/shard_map/scores/pallas_call | solution.py:102
  31.1 0.0 collective-permute-done.3.refs_4_
  31.1 0.0 collective-permute-done.2.refs_2_
  31.1 0.2 collective-permute-start.8
  31.3 0.4 %collective-permute-start.9 = (bf16[128,1024]{1,0:T(8,128)(2,1)S(1)}, bf16[128,1024]{1,0:T(8,128)(2,1)S(1)}, u32[]{:S(2)}, u32[]{:S(2)}) collective-permute-start(bf16[128,1024]{1,0:T(8,128)(2,1)S(1)} %collective-permute-done.3.refs_4_), channel_id=1, source_target_pairs={{0,1},{1,0},{2,3},{3,2},{4,5},{5,4},{6,7},{7,6},{8,9},{9,8},{10,11... | collective-permute-start | bytes 786440 | tf_op jit(solution)/shard_map/ppermute | solution.py:156
  31.7 0.0 collective-permute-done.7.refs_1_
  31.7 1.0 %collective-permute-done.8.refs_3_ = bf16[128,1024]{1,0:T(8,128)(2,1)S(1)} collective-permute-done((bf16[128,1024]{1,0:T(8,128)(2,1)S(1)}, bf16[128,1024]{1,0:T(8,128)(2,1)S(1)}, u32[]{:S(2)}, u32[]{:S(2)}) %collective-permute-start.8) | collective-permute-done | bytes 262176 | tf_op jit(solution)/shard_map/ppermute | solution.py:156
  32.7 0.4 %collective-permute-done.9.refs_5_ = bf16[128,1024]{1,0:T(8,128)(2,1)S(1)} collective-permute-done((bf16[128,1024]{1,0:T(8,128)(2,1)S(1)}, bf16[128,1024]{1,0:T(8,128)(2,1)S(1)}, u32[]{:S(2)}, u32[]{:S(2)}) %collective-permute-start.9) | collective-permute-done | bytes 262176 | tf_op jit(solution)/shard_map/ppermute | solution.py:156
  33.1 0.0 copy-done
  33.1 2.7 %values.1 = bf16[128,4096]{1,0:T(8,128)(2,1)} custom-call(s32[2]{0:T(128)S(1)} %pad_add_fusion.here_ref, bf16[4096,512]{1,0:T(8,128)(2,1)S(1)} %get-tuple-element.23.weight_ref, f32[32,128]{1,0:T(8,128)S(1)} %get-tuple-element.24.inverse_ref, bf16[128,1024]{1,0:T(8,128)(2,1)S(1)} %copy-done, bf16[128,1024]{1,0:T(8,128)(2,1)S(1)} %collective-permute-done.7.refs_1_, ...), custom_call_target="tpu_custom_call" | custom-call | flops 671088640 | bytes 8388608 | tf_op jit(solution)/shard_map/values/pallas_call | solution.py:127
Async XLA Ops:
  0.6 32.5 %copy-start = (bf16[128,1024]{1,0:T(8,128)(2,1)S(1)}, bf16[128,1024]{1,0:T(8,128)(2,1)}, u32[]{:S(2)}) copy-start(bf16[128,1024]{1,0:T(8,128)(2,1)} %refs_0_.3) | copy-start | bytes 786436
  0.6 12.3 %collective-permute-start.5 = (bf16[128,1024]{1,0:T(8,128)(2,1)}, bf16[128,1024]{1,0:T(8,128)(2,1)S(1)}, u32[]{:S(2)}, u32[]{:S(2)}) collective-permute-start(bf16[128,1024]{1,0:T(8,128)(2,1)} %refs_0_.2), channel_id=1, source_target_pairs={{0,2},{1,3},{2,4},{3,5},{4,6},{5,7},{6,8},{7,9},{8,10},{9,11},{10,... | collective-permute-start | bytes 786440 | tf_op jit(solution)/shard_map/ppermute | solution.py:150
  1.9 16.3 %collective-permute-start.6 = (bf16[128,1024]{1,0:T(8,128)(2,1)}, bf16[128,1024]{1,0:T(8,128)(2,1)S(1)}, u32[]{:S(2)}, u32[]{:S(2)}) collective-permute-start(bf16[128,1024]{1,0:T(8,128)(2,1)} %refs_0_.2), channel_id=1, source_target_pairs={{0,4},{1,5},{2,6},{3,7},{4,8},{5,9},{6,10},{7,11},{8,12},{9,13},{1... | collective-permute-start | bytes 786440 | tf_op jit(solution)/shard_map/ppermute | solution.py:153
  6.3 16.8 %collective-permute-start.4 = (bf16[128,1024]{1,0:T(8,128)(2,1)}, bf16[128,1024]{1,0:T(8,128)(2,1)S(1)}, u32[]{:S(2)}, u32[]{:S(2)}) collective-permute-start(bf16[128,1024]{1,0:T(8,128)(2,1)} %refs_0_.2), channel_id=1, source_target_pairs={{0,1},{1,0},{2,3},{3,2},{4,5},{5,4},{6,7},{7,6},{8,9},{9,8},{10,11... | collective-permute-start | bytes 786440 | tf_op jit(solution)/shard_map/ppermute | solution.py:156
  7.6 23.5 %collective-permute-start.3 = (bf16[128,1024]{1,0:T(8,128)(2,1)}, bf16[128,1024]{1,0:T(8,128)(2,1)S(1)}, u32[]{:S(2)}, u32[]{:S(2)}) collective-permute-start(bf16[128,1024]{1,0:T(8,128)(2,1)} %refs_0_.3), channel_id=1, source_target_pairs={{0,4},{1,5},{2,6},{3,7},{4,8},{5,9},{6,10},{7,11},{8,12},{9,13},{1... | collective-permute-start | bytes 786440 | tf_op jit(solution)/shard_map/ppermute | solution.py:153
  11.0 20.1 %collective-permute-start.2 = (bf16[128,1024]{1,0:T(8,128)(2,1)}, bf16[128,1024]{1,0:T(8,128)(2,1)S(1)}, u32[]{:S(2)}, u32[]{:S(2)}) collective-permute-start(bf16[128,1024]{1,0:T(8,128)(2,1)} %refs_0_.3), channel_id=1, source_target_pairs={{0,2},{1,3},{2,4},{3,5},{4,6},{5,7},{6,8},{7,9},{8,10},{9,11},{10,... | collective-permute-start | bytes 786440 | tf_op jit(solution)/shard_map/ppermute | solution.py:150
  18.2 4.1 %collective-permute-start = (bf16[128,1024]{1,0:T(8,128)(2,1)S(1)}, bf16[128,1024]{1,0:T(8,128)(2,1)}, u32[]{:S(2)}, u32[]{:S(2)}) collective-permute-start(bf16[128,1024]{1,0:T(8,128)(2,1)S(1)} %get-tuple-element.8), channel_id=1, source_target_pairs={{0,1},{1,0},{2,3},{3,2},{4,5},{5,4},{6,7},{7,6},{8,9},{9,8},{10,11... | collective-permute-start | bytes 786440 | tf_op jit(solution)/shard_map/cond/branch_1_fun/ppermute | solution.py:156
  21.0 1.7 %collective-permute-start.1 = (bf16[128,1024]{1,0:T(8,128)(2,1)S(1)}, bf16[128,1024]{1,0:T(8,128)(2,1)}, u32[]{:S(2)}, u32[]{:S(2)}) collective-permute-start(bf16[128,1024]{1,0:T(8,128)(2,1)S(1)} %get-tuple-element.9), channel_id=1, source_target_pairs={{0,1},{1,0},{2,3},{3,2},{4,5},{5,4},{6,7},{7,6},{8,9},{9,8},{10,11... | collective-permute-start | bytes 786440 | tf_op jit(solution)/shard_map/cond/branch_1_fun/ppermute | solution.py:156
  22.7 9.0 %collective-permute-start.7 = (bf16[128,1024]{1,0:T(8,128)(2,1)}, bf16[128,1024]{1,0:T(8,128)(2,1)S(1)}, u32[]{:S(2)}, u32[]{:S(2)}) collective-permute-start(bf16[128,1024]{1,0:T(8,128)(2,1)} %refs_0_.3), channel_id=1, source_target_pairs={{0,1},{1,0},{2,3},{3,2},{4,5},{5,4},{6,7},{7,6},{8,9},{9,8},{10,11... | collective-permute-start | bytes 786440 | tf_op jit(solution)/shard_map/ppermute | solution.py:156
  23.1 1.2 %copy-start.1 = (bf16[128,4096]{1,0:T(8,128)(2,1)S(1)}, bf16[128,4096]{1,0:T(8,128)(2,1)}, u32[]{:S(2)}) copy-start(bf16[128,4096]{1,0:T(8,128)(2,1)} %q_ref.1) | copy-start | bytes 3145732
  24.3 0.9 %copy-start.2 = (bf16[128,1024]{1,0:T(8,128)(2,1)S(1)}, bf16[128,1024]{1,0:T(8,128)(2,1)}, u32[]{:S(2)}) copy-start(bf16[128,1024]{1,0:T(8,128)(2,1)} %refs_0_.2) | copy-start | bytes 786436
  25.3 0.7 %copy-start.3 = (s32[128]{0:T(128)S(1)}, s32[128]{0:T(128)}, u32[]{:S(2)}) copy-start(s32[128]{0:T(128)} %param.9) | copy-start | bytes 1540
  31.1 1.6 %collective-permute-start.8 = (bf16[128,1024]{1,0:T(8,128)(2,1)S(1)}, bf16[128,1024]{1,0:T(8,128)(2,1)S(1)}, u32[]{:S(2)}, u32[]{:S(2)}) collective-permute-start(bf16[128,1024]{1,0:T(8,128)(2,1)S(1)} %collective-permute-done.2.refs_2_), channel_id=1, source_target_pairs={{0,1},{1,0},{2,3},{3,2},{4,5},{5,4},{6,7},{7,6},{8,9},{9,8},{10,11... | collective-permute-start | bytes 786440 | tf_op jit(solution)/shard_map/ppermute | solution.py:156
  31.3 1.8 %collective-permute-start.9 = (bf16[128,1024]{1,0:T(8,128)(2,1)S(1)}, bf16[128,1024]{1,0:T(8,128)(2,1)S(1)}, u32[]{:S(2)}, u32[]{:S(2)}) collective-permute-start(bf16[128,1024]{1,0:T(8,128)(2,1)S(1)} %collective-permute-done.3.refs_4_), channel_id=1, source_target_pairs={{0,1},{1,0},{2,3},{3,2},{4,5},{5,4},{6,7},{7,6},{8,9},{9,8},{10,11... | collective-permute-start | bytes 786440 | tf_op jit(solution)/shard_map/ppermute | solution.py:156

commit v2 on v1

--- a/solution.py
+++ b/solution.py
@@ -30,17 +30,35 @@
     return jnp.concatenate([own, four, one, two, three], axis=0)
 
 
-def scores_kernel(pairs, group, here_ref, doc_ref, q_ref, *refs):
-    blocks, (weight_ref, inverse_ref, log_ref, bias_ref) = refs[:6], refs[6:]
+def scores_kernel(
+    pairs, group, here_ref, near, two, four, doc_hbm, q_hbm, own_hbm, two_swap_hbm, four_swap_hbm,
+    weight_ref, inverse_ref, log_ref, doc_ref, q_ref, own, two_swap, four_swap, bias_ref, sems,
+):
+    moves = [
+        (doc_hbm, doc_ref),
+        (own_hbm, own),
+        (two_swap_hbm, two_swap),
+        (four_swap_hbm, four_swap),
+        (q_hbm, q_ref),
+    ]
+    copies = [
+        pltpu.make_async_copy(source, target, sems.at[index])
+        for index, (source, target) in enumerate(moves)
+    ]
+    for copy in copies:
+        copy.start()
     rows = q_ref.shape[0]
     causal, place = causal_tile(rows)
-
+    copies[0].wait()
     start = jnp.broadcast_to(doc_ref[...] - here_ref[0], (rows, rows))
     merged = jnp.where(causal, place, place - BACK * rows)
     bias_ref[0] = jnp.where(merged >= start, 0.0, LOWEST)
     for back in range(1, BACK):
         bias_ref[back] = jnp.where(place - back * rows >= start, 0.0, LOWEST)
-
+    for copy in copies[1:]:
+        copy.wait()
+
+    blocks = (own, near, two, two_swap, four, four_swap)
     for pair in range(pairs):
         key = in_order(here_ref, blocks, slice(pair * HEAD_DIM, (pair + 1) * HEAD_DIM))
         for g in range(group):
@@ -68,8 +86,9 @@
 
 
 def values_kernel(pairs, group, here_ref, weight_ref, inverse_ref, *refs):
-    blocks, out_ref = refs[:6], refs[6]
+    blocks, (out_hbm, out_ref, sems) = refs[:6], refs[6:]
     rows = out_ref.shape[0]
+    copies = []
     causal, _ = causal_tile(rows)
     causal = jnp.concatenate([causal] * group, axis=1)
     for pair in range(pairs):
@@ -90,6 +109,13 @@
                     out_ref.dtype
                 )
             )
+        part = pl.ds(pair * group * HEAD_DIM, group * HEAD_DIM)
+        copies.append(
+            pltpu.make_async_copy(out_ref.at[:, part], out_hbm.at[:, part], sems.at[pair])
+        )
+        copies[-1].start()
+    for copy in copies:
+        copy.wait()
 
 
 def weigh(queries, keys, doc_start, here):
@@ -99,16 +125,20 @@
     heads = kv_heads * group
     reach = BACK * rows
     whole = pl.BlockSpec(memory_space=pltpu.VMEM)
+    left = pl.BlockSpec(memory_space=pltpu.HBM)
+    own, near, two, two_swap, four, four_swap = keys
+    brought = [doc_start.reshape(1, rows), queries, own, two_swap, four_swap]
     return pl.pallas_call(
         functools.partial(scores_kernel, kv_heads, group),
-        in_specs=[pl.BlockSpec(memory_space=pltpu.SMEM)] + [whole] * 8,
+        in_specs=[pl.BlockSpec(memory_space=pltpu.SMEM)] + [whole] * 3 + [left] * 5,
         out_specs=[whole] * 3,
         out_shape=[
             jax.ShapeDtypeStruct((kv_heads * reach, group * rows), jnp.bfloat16),
             jax.ShapeDtypeStruct((heads, rows), jnp.float32),
             jax.ShapeDtypeStruct((heads, rows), jnp.float32),
         ],
-        scratch_shapes=[pltpu.VMEM((BACK, rows, rows), jnp.float32)],
+        scratch_shapes=[pltpu.VMEM(x.shape, x.dtype) for x in brought]
+        + [pltpu.VMEM((BACK, rows, rows), jnp.float32), pltpu.SemaphoreType.DMA((5,))],
         cost_estimate=pl.CostEstimate(
             flops=2 * rows * (reach + rows) * width,
             bytes_accessed=8 << 20,
@@ -116,7 +146,13 @@
         ),
         compiler_params=pltpu.CompilerParams(vmem_limit_bytes=32 << 20),
         name="scores",
-    )(here, doc_start.reshape(1, rows), queries, *keys)
+    )(
+        here,
+        near,
+        two,
+        four,
+        *[pltpu.with_memory_space_constraint(x, pltpu.HBM) for x in brought],
+    )
 
 
 def combine(weights, inverses, values, here, width):
@@ -127,8 +163,12 @@
     return pl.pallas_call(
         functools.partial(values_kernel, kv_heads, group),
         in_specs=[pl.BlockSpec(memory_space=pltpu.SMEM)] + [whole] * 8,
-        out_specs=whole,
+        out_specs=pl.BlockSpec(memory_space=pltpu.HBM),
         out_shape=jax.ShapeDtypeStruct((rows, width), jnp.bfloat16),
+        scratch_shapes=[
+            pltpu.VMEM((rows, width), jnp.bfloat16),
+            pltpu.SemaphoreType.DMA((kv_heads,)),
+        ],
         cost_estimate=pl.CostEstimate(
             flops=2 * rows * (BACK + 1) * rows * width, bytes_accessed=8 << 20, transcendentals=0
         ),
@@ -144,8 +184,8 @@
     here = jnp.stack([me * rows, me % 2]).astype(jnp.int32)
     chain = devices - BACK
 
-    def two_back(x):
-        pairs = [(i, (i + 2) % chain) for i in range(chain)]
+    def shifted(x, by):
+        pairs = [(i, (i + by) % chain) for i in range(chain)]
         pairs += [(chain + i, chain + (i + 2) % BACK) for i in range(BACK)]
         return lax.ppermute(x, AXES, pairs)
 
@@ -156,8 +196,8 @@
         return lax.ppermute(x, AXES, [(i, i ^ 1) for i in range(devices)])
 
     key_near = swapped(keys)
-    key_two, key_four = two_back(keys), four_back(keys)
-    value_two, value_four = two_back(values), four_back(values)
+    key_two, key_four = shifted(keys, 2), four_back(keys)
+    value_two, value_four = shifted(values, 2), four_back(values)
     value_near = swapped(values)
     key_two_swap, key_four_swap = lax.cond(
         doc_start[0] >= 0,

time: 36.1 us -> 35.3 us (0.978)
  local copies, waits for them, and re-layouts: 2.84 us -> 0.01 us
  waiting for transfers between devices: 8.29 us -> 9.61 us
  Pallas kernels: 7.9 us -> 8.73 us
    unnamed x8 -> x2, local copies, waits for them, and re-layouts: 2.84 us -> 0.01 us
    ppermute x2, waiting for transfers between devices: 0.01 us -> 1.23 us  [shifted(): return lax.ppermute(x, AXES, pairs)]
    pallas_call x1, Pallas kernels: 5.16 us -> 6.16 us  [weigh(): pl.pallas_call(functools.partial(scores_kernel, kv_heads, group), in_spec...]
  transfers between devices with their start and end apart: 10 -> 10, of which waited for: 5 -> 6; matrix products, arithmetic and copies ran while one was open for 0% -> 0% of each run, Pallas kernels for 14% -> 18%
where the time goes in v2:
time: 35.3 us; the launch traced here: 35.1 us
  starting transfers between devices  15.3 us (43%)
  waiting for transfers between devices  9.61 us (27%)
  Pallas kernels  8.73 us (25%)
  between operations  1.34 us (4%)
    ppermute x2, starting transfers between devices, four_back(): return lax.ppermute(x, AXES, [(i, i + 4) for i in range(chain - 4)])  7.78 us
    pallas_call x1, Pallas kernels, weigh(): pl.pallas_call(functools.partial(scores_kernel, kv_heads, group), in_spec...  6.16 us
    ppermute x2, waiting for transfers between devices, four_back(): return lax.ppermute(x, AXES, [(i, i + 4) for i in range(chain - 4)])  5.22 us
    ppermute x6, starting transfers between devices, swapped(): return lax.ppermute(x, AXES, [(i, i ^ 1) for i in range(devices)])  4.99 us
    ppermute x6, waiting for transfers between devices, swapped(): return lax.ppermute(x, AXES, [(i, i ^ 1) for i in range(devices)])  3.16 us
    pallas_call x1, Pallas kernels, combine(): pl.pallas_call(functools.partial(values_kernel, kv_heads, group), in_spec...  2.57 us
    ppermute x2, starting transfers between devices, shifted(): return lax.ppermute(x, AXES, pairs)  2.56 us
    ppermute x2, waiting for transfers between devices, shifted(): return lax.ppermute(x, AXES, pairs)  1.23 us
  transfers between devices with their start and end apart: 10, of which 6 were waited for; matrix products, arithmetic and copies ran while one was open for 0% of the time, Pallas kernels for 18%

profile of v2, /device:TPU:97, one launch (start us, length us, event | category | flops | bytes accessed | tf_op | source)
XLA Modules:
  0.0 35.1 jit_solution(10270169748166155986)
XLA Ops:
  0.6 0.0 copy-start
  0.6 1.3 %collective-permute-start.5 = (bf16[128,1024]{1,0:T(8,128)(2,1)}, bf16[128,1024]{1,0:T(8,128)(2,1)S(1)}, u32[]{:S(2)}, u32[]{:S(2)}) collective-permute-start(bf16[128,1024]{1,0:T(8,128)(2,1)} %own_hbm.1), channel_id=1, source_target_pairs={{0,2},{1,3},{2,4},{3,5},{4,6},{5,7},{6,8},{7,9},{8,10},{9,11},{10,... | collective-permute-start | bytes 786440 | tf_op jit(solution)/shard_map/ppermute | solution.py:190
  1.9 4.3 %collective-permute-start.6 = (bf16[128,1024]{1,0:T(8,128)(2,1)}, bf16[128,1024]{1,0:T(8,128)(2,1)S(1)}, u32[]{:S(2)}, u32[]{:S(2)}) collective-permute-start(bf16[128,1024]{1,0:T(8,128)(2,1)} %own_hbm.1), channel_id=1, source_target_pairs={{0,4},{1,5},{2,6},{3,7},{4,8},{5,9},{6,10},{7,11},{8,12},{9,13},{1... | collective-permute-start | bytes 786440 | tf_op jit(solution)/shard_map/ppermute | solution.py:193
  6.3 1.3 %collective-permute-start.4 = (bf16[128,1024]{1,0:T(8,128)(2,1)}, bf16[128,1024]{1,0:T(8,128)(2,1)S(1)}, u32[]{:S(2)}, u32[]{:S(2)}) collective-permute-start(bf16[128,1024]{1,0:T(8,128)(2,1)} %own_hbm.1), channel_id=1, source_target_pairs={{0,1},{1,0},{2,3},{3,2},{4,5},{5,4},{6,7},{7,6},{8,9},{9,8},{10,11... | collective-permute-start | bytes 786440 | tf_op jit(solution)/shard_map/ppermute | solution.py:196
  7.6 3.4 %collective-permute-start.3 = (bf16[128,1024]{1,0:T(8,128)(2,1)}, bf16[128,1024]{1,0:T(8,128)(2,1)S(1)}, u32[]{:S(2)}, u32[]{:S(2)}) collective-permute-start(bf16[128,1024]{1,0:T(8,128)(2,1)} %refs_0_.1), channel_id=1, source_target_pairs={{0,4},{1,5},{2,6},{3,7},{4,8},{5,9},{6,10},{7,11},{8,12},{9,13},{1... | collective-permute-start | bytes 786440 | tf_op jit(solution)/shard_map/ppermute | solution.py:193
  11.0 1.3 %collective-permute-start.2 = (bf16[128,1024]{1,0:T(8,128)(2,1)}, bf16[128,1024]{1,0:T(8,128)(2,1)S(1)}, u32[]{:S(2)}, u32[]{:S(2)}) collective-permute-start(bf16[128,1024]{1,0:T(8,128)(2,1)} %refs_0_.1), channel_id=1, source_target_pairs={{0,2},{1,3},{2,4},{3,5},{4,6},{5,7},{6,8},{7,9},{8,10},{9,11},{10,... | collective-permute-start | bytes 786440 | tf_op jit(solution)/shard_map/ppermute | solution.py:190
  13.0 0.0 collective-permute-done.5.two
  13.0 5.2 %collective-permute-done.6.four = bf16[128,1024]{1,0:T(8,128)(2,1)S(1)} collective-permute-done((bf16[128,1024]{1,0:T(8,128)(2,1)}, bf16[128,1024]{1,0:T(8,128)(2,1)S(1)}, u32[]{:S(2)}, u32[]{:S(2)}) %collective-permute-start.6) | collective-permute-done | bytes 262176 | tf_op jit(solution)/shard_map/ppermute | solution.py:193
  18.2 4.5 %conditional.1 = (bf16[128,1024]{1,0:T(8,128)(2,1)}, bf16[128,1024]{1,0:T(8,128)(2,1)}) conditional(s32[]{:T(128)} %bitcast.3, (bf16[128,1024]{1,0:T(8,128)(2,1)S(1)}, bf16[128,1024]{1,0:T(8,128)(2,1)S(1)}) %tuple.16, (bf16[128,1024]{1,0:T(8,128)(2,1)S(1)}, bf16[128,1024]{1,0:T(8,128)(2,1)S(1)}) %tuple.16), branch_computations={%region_0.1_spmd, %region_1.2_spmd} | conditional | bytes 2097248 | solution.py:202
  18.2 2.8 %collective-permute-start = (bf16[128,1024]{1,0:T(8,128)(2,1)S(1)}, bf16[128,1024]{1,0:T(8,128)(2,1)}, u32[]{:S(2)}, u32[]{:S(2)}) collective-permute-start(bf16[128,1024]{1,0:T(8,128)(2,1)S(1)} %get-tuple-element.8), channel_id=1, source_target_pairs={{0,1},{1,0},{2,3},{3,2},{4,5},{5,4},{6,7},{7,6},{8,9},{9,8},{10,11... | collective-permute-start | bytes 786440 | tf_op jit(solution)/shard_map/cond/branch_1_fun/ppermute | solution.py:196
  21.0 0.0 collective-permute-start.1
  21.0 1.3 %collective-permute-done = bf16[128,1024]{1,0:T(8,128)(2,1)} collective-permute-done((bf16[128,1024]{1,0:T(8,128)(2,1)S(1)}, bf16[128,1024]{1,0:T(8,128)(2,1)}, u32[]{:S(2)}, u32[]{:S(2)}) %collective-permute-start) | collective-permute-done | bytes 262176 | tf_op jit(solution)/shard_map/cond/branch_1_fun/ppermute | solution.py:196
  22.3 0.4 %collective-permute-done.1 = bf16[128,1024]{1,0:T(8,128)(2,1)} collective-permute-done((bf16[128,1024]{1,0:T(8,128)(2,1)S(1)}, bf16[128,1024]{1,0:T(8,128)(2,1)}, u32[]{:S(2)}, u32[]{:S(2)}) %collective-permute-start.1) | collective-permute-done | bytes 262176 | tf_op jit(solution)/shard_map/cond/branch_1_fun/ppermute | solution.py:196
  22.7 0.4 %collective-permute-start.7 = (bf16[128,1024]{1,0:T(8,128)(2,1)}, bf16[128,1024]{1,0:T(8,128)(2,1)S(1)}, u32[]{:S(2)}, u32[]{:S(2)}) collective-permute-start(bf16[128,1024]{1,0:T(8,128)(2,1)} %refs_0_.1), channel_id=1, source_target_pairs={{0,1},{1,0},{2,3},{3,2},{4,5},{5,4},{6,7},{7,6},{8,9},{9,8},{10,11... | collective-permute-start | bytes 786440 | tf_op jit(solution)/shard_map/ppermute | solution.py:196
  23.0 0.1 pad_add_fusion.here_ref
  23.1 0.0 collective-permute-done.4.near
  23.1 6.2 %scores.1 = (bf16[4096,512]{1,0:T(8,128)(2,1)S(1)}, f32[32,128]{1,0:T(8,128)S(1)}, f32[32,128]{1,0:T(8,128)}) custom-call(s32[2]{0:T(128)S(1)} %pad_add_fusion.here_ref, bf16[128,1024]{1,0:T(8,128)(2,1)S(1)} %collective-permute-done.4.near, bf16[128,1024]{1,0:T(8,128)(2,1)S(1)} %collective-permute-done.5.two, ...), custom_call_target="tpu_custom_call" | custom-call | flops 671088640 | bytes 8388608 | tf_op jit(solution)/shard_map/scores/pallas_call | solution.py:131
  29.3 0.0 collective-permute-done.3.refs_4_
  29.3 1.2 %collective-permute-done.2.refs_2_ = bf16[128,1024]{1,0:T(8,128)(2,1)S(1)} collective-permute-done((bf16[128,1024]{1,0:T(8,128)(2,1)}, bf16[128,1024]{1,0:T(8,128)(2,1)S(1)}, u32[]{:S(2)}, u32[]{:S(2)}) %collective-permute-start.2) | collective-permute-done | bytes 262176 | tf_op jit(solution)/shard_map/ppermute | solution.py:190
  30.5 0.5 %collective-permute-start.8 = (bf16[128,1024]{1,0:T(8,128)(2,1)S(1)}, bf16[128,1024]{1,0:T(8,128)(2,1)S(1)}, u32[]{:S(2)}, u32[]{:S(2)}) collective-permute-start(bf16[128,1024]{1,0:T(8,128)(2,1)S(1)} %collective-permute-done.2.refs_2_), channel_id=1, source_target_pairs={{0,1},{1,0},{2,3},{3,2},{4,5},{5,4},{6,7},{7,6},{8,9},{9,8},{10,11... | collective-permute-start | bytes 786440 | tf_op jit(solution)/shard_map/ppermute | solution.py:196
  31.0 0.0 collective-permute-start.9
  31.0 0.0 collective-permute-done.7.refs_1_
  31.0 1.1 %collective-permute-done.8.refs_3_ = bf16[128,1024]{1,0:T(8,128)(2,1)S(1)} collective-permute-done((bf16[128,1024]{1,0:T(8,128)(2,1)S(1)}, bf16[128,1024]{1,0:T(8,128)(2,1)S(1)}, u32[]{:S(2)}, u32[]{:S(2)}) %collective-permute-start.8) | collective-permute-done | bytes 262176 | tf_op jit(solution)/shard_map/ppermute | solution.py:196
  32.1 0.4 %collective-permute-done.9.refs_5_ = bf16[128,1024]{1,0:T(8,128)(2,1)S(1)} collective-permute-done((bf16[128,1024]{1,0:T(8,128)(2,1)S(1)}, bf16[128,1024]{1,0:T(8,128)(2,1)S(1)}, u32[]{:S(2)}, u32[]{:S(2)}) %collective-permute-start.9) | collective-permute-done | bytes 262176 | tf_op jit(solution)/shard_map/ppermute | solution.py:196
  32.5 0.0 copy-done
  32.5 2.6 %values.1 = bf16[128,4096]{1,0:T(8,128)(2,1)} custom-call(s32[2]{0:T(128)S(1)} %pad_add_fusion.here_ref, bf16[4096,512]{1,0:T(8,128)(2,1)S(1)} %get-tuple-element.23.weight_ref, f32[32,128]{1,0:T(8,128)S(1)} %get-tuple-element.24.inverse_ref, bf16[128,1024]{1,0:T(8,128)(2,1)S(1)} %copy-done, bf16[128,1024]{1,0:T(8,128)(2,1)S(1)} %collective-permute-done.7.refs_1_, ...), custom_call_target="tpu_custom_call" | custom-call | flops 671088640 | bytes 8388608 | tf_op jit(solution)/shard_map/values/pallas_call | solution.py:163
Async XLA Ops:
  0.6 31.9 %copy-start = (bf16[128,1024]{1,0:T(8,128)(2,1)S(1)}, bf16[128,1024]{1,0:T(8,128)(2,1)}, u32[]{:S(2)}) copy-start(bf16[128,1024]{1,0:T(8,128)(2,1)} %refs_0_.1) | copy-start | bytes 786436
  0.6 12.3 %collective-permute-start.5 = (bf16[128,1024]{1,0:T(8,128)(2,1)}, bf16[128,1024]{1,0:T(8,128)(2,1)S(1)}, u32[]{:S(2)}, u32[]{:S(2)}) collective-permute-start(bf16[128,1024]{1,0:T(8,128)(2,1)} %own_hbm.1), channel_id=1, source_target_pairs={{0,2},{1,3},{2,4},{3,5},{4,6},{5,7},{6,8},{7,9},{8,10},{9,11},{10,... | collective-permute-start | bytes 786440 | tf_op jit(solution)/shard_map/ppermute | solution.py:190
  1.9 16.3 %collective-permute-start.6 = (bf16[128,1024]{1,0:T(8,128)(2,1)}, bf16[128,1024]{1,0:T(8,128)(2,1)S(1)}, u32[]{:S(2)}, u32[]{:S(2)}) collective-permute-start(bf16[128,1024]{1,0:T(8,128)(2,1)} %own_hbm.1), channel_id=1, source_target_pairs={{0,4},{1,5},{2,6},{3,7},{4,8},{5,9},{6,10},{7,11},{8,12},{9,13},{1... | collective-permute-start | bytes 786440 | tf_op jit(solution)/shard_map/ppermute | solution.py:193
  6.3 16.8 %collective-permute-start.4 = (bf16[128,1024]{1,0:T(8,128)(2,1)}, bf16[128,1024]{1,0:T(8,128)(2,1)S(1)}, u32[]{:S(2)}, u32[]{:S(2)}) collective-permute-start(bf16[128,1024]{1,0:T(8,128)(2,1)} %own_hbm.1), channel_id=1, source_target_pairs={{0,1},{1,0},{2,3},{3,2},{4,5},{5,4},{6,7},{7,6},{8,9},{9,8},{10,11... | collective-permute-start | bytes 786440 | tf_op jit(solution)/shard_map/ppermute | solution.py:196
  7.6 21.7 %collective-permute-start.3 = (bf16[128,1024]{1,0:T(8,128)(2,1)}, bf16[128,1024]{1,0:T(8,128)(2,1)S(1)}, u32[]{:S(2)}, u32[]{:S(2)}) collective-permute-start(bf16[128,1024]{1,0:T(8,128)(2,1)} %refs_0_.1), channel_id=1, source_target_pairs={{0,4},{1,5},{2,6},{3,7},{4,8},{5,9},{6,10},{7,11},{8,12},{9,13},{1... | collective-permute-start | bytes 786440 | tf_op jit(solution)/shard_map/ppermute | solution.py:193
  11.0 19.5 %collective-permute-start.2 = (bf16[128,1024]{1,0:T(8,128)(2,1)}, bf16[128,1024]{1,0:T(8,128)(2,1)S(1)}, u32[]{:S(2)}, u32[]{:S(2)}) collective-permute-start(bf16[128,1024]{1,0:T(8,128)(2,1)} %refs_0_.1), channel_id=1, source_target_pairs={{0,2},{1,3},{2,4},{3,5},{4,6},{5,7},{6,8},{7,9},{8,10},{9,11},{10,... | collective-permute-start | bytes 786440 | tf_op jit(solution)/shard_map/ppermute | solution.py:190
  18.2 4.1 %collective-permute-start = (bf16[128,1024]{1,0:T(8,128)(2,1)S(1)}, bf16[128,1024]{1,0:T(8,128)(2,1)}, u32[]{:S(2)}, u32[]{:S(2)}) collective-permute-start(bf16[128,1024]{1,0:T(8,128)(2,1)S(1)} %get-tuple-element.8), channel_id=1, source_target_pairs={{0,1},{1,0},{2,3},{3,2},{4,5},{5,4},{6,7},{7,6},{8,9},{9,8},{10,11... | collective-permute-start | bytes 786440 | tf_op jit(solution)/shard_map/cond/branch_1_fun/ppermute | solution.py:196
  21.0 1.7 %collective-permute-start.1 = (bf16[128,1024]{1,0:T(8,128)(2,1)S(1)}, bf16[128,1024]{1,0:T(8,128)(2,1)}, u32[]{:S(2)}, u32[]{:S(2)}) collective-permute-start(bf16[128,1024]{1,0:T(8,128)(2,1)S(1)} %get-tuple-element.9), channel_id=1, source_target_pairs={{0,1},{1,0},{2,3},{3,2},{4,5},{5,4},{6,7},{7,6},{8,9},{9,8},{10,11... | collective-permute-start | bytes 786440 | tf_op jit(solution)/shard_map/cond/branch_1_fun/ppermute | solution.py:196
  22.7 8.4 %collective-permute-start.7 = (bf16[128,1024]{1,0:T(8,128)(2,1)}, bf16[128,1024]{1,0:T(8,128)(2,1)S(1)}, u32[]{:S(2)}, u32[]{:S(2)}) collective-permute-start(bf16[128,1024]{1,0:T(8,128)(2,1)} %refs_0_.1), channel_id=1, source_target_pairs={{0,1},{1,0},{2,3},{3,2},{4,5},{5,4},{6,7},{7,6},{8,9},{9,8},{10,11... | collective-permute-start | bytes 786440 | tf_op jit(solution)/shard_map/ppermute | solution.py:196
  30.5 1.6 %collective-permute-start.8 = (bf16[128,1024]{1,0:T(8,128)(2,1)S(1)}, bf16[128,1024]{1,0:T(8,128)(2,1)S(1)}, u32[]{:S(2)}, u32[]{:S(2)}) collective-permute-start(bf16[128,1024]{1,0:T(8,128)(2,1)S(1)} %collective-permute-done.2.refs_2_), channel_id=1, source_target_pairs={{0,1},{1,0},{2,3},{3,2},{4,5},{5,4},{6,7},{7,6},{8,9},{9,8},{10,11... | collective-permute-start | bytes 786440 | tf_op jit(solution)/shard_map/ppermute | solution.py:196
  31.0 1.5 %collective-permute-start.9 = (bf16[128,1024]{1,0:T(8,128)(2,1)S(1)}, bf16[128,1024]{1,0:T(8,128)(2,1)S(1)}, u32[]{:S(2)}, u32[]{:S(2)}) collective-permute-start(bf16[128,1024]{1,0:T(8,128)(2,1)S(1)} %collective-permute-done.3.refs_4_), channel_id=1, source_target_pairs={{0,1},{1,0},{2,3},{3,2},{4,5},{5,4},{6,7},{7,6},{8,9},{9,8},{10,11... | collective-permute-start | bytes 786440 | tf_op jit(solution)/shard_map/ppermute | solution.py:196

commit v3 on v2

--- a/solution.py
+++ b/solution.py
@@ -208,9 +208,11 @@
     )
     all_keys = (keys, key_near, key_two, key_two_swap, key_four, key_four_swap)
     weights, inverses, logs = weigh(queries, all_keys, doc_start, here)
-    value_two, value_four, weights = lax.optimization_barrier((value_two, value_four, weights))
+    value_four, weights = lax.optimization_barrier((value_four, weights))
+    value_four_swap = swapped(value_four)
+    value_two, value_four_swap = lax.optimization_barrier((value_two, value_four_swap))
     all_values = (
-        values, value_near, value_two, swapped(value_two), value_four, swapped(value_four)
+        values, value_near, value_two, swapped(value_two), value_four, value_four_swap
     )
     return combine(weights, inverses, all_values, here, width), logs
 

time: 35.3 us -> 34.9 us (0.989)
  waiting for transfers between devices: 9.61 us -> 9.02 us
  transfers between devices with their start and end apart: 10 -> 10, of which waited for: 6 -> 5; matrix products, arithmetic and copies ran while one was open for 0% -> 0% of each run, Pallas kernels for 18% -> 18%
where the time goes in v3:
time: 34.9 us; the launch traced here: 34.7 us
  starting transfers between devices  15.5 us (44%)
  waiting for transfers between devices  9.02 us (26%)
  Pallas kernels  8.78 us (25%)
  between operations  1.33 us (4%)
    ppermute x2, starting transfers between devices, four_back(): return lax.ppermute(x, AXES, [(i, i + 4) for i in range(chain - 4)])  7.78 us
    pallas_call x1, Pallas kernels, weigh(): pl.pallas_call(functools.partial(scores_kernel, kv_heads, group), in_spec...  6.21 us
    ppermute x6, starting transfers between devices, swapped(): return lax.ppermute(x, AXES, [(i, i ^ 1) for i in range(devices)])  5.17 us
    ppermute x2, waiting for transfers between devices, four_back(): return lax.ppermute(x, AXES, [(i, i + 4) for i in range(chain - 4)])  5.15 us
    ppermute x6, waiting for transfers between devices, swapped(): return lax.ppermute(x, AXES, [(i, i ^ 1) for i in range(devices)])  2.83 us
    pallas_call x1, Pallas kernels, combine(): pl.pallas_call(functools.partial(values_kernel, kv_heads, group), in_spec...  2.57 us
    ppermute x2, starting transfers between devices, shifted(): return lax.ppermute(x, AXES, pairs)  2.56 us
    ppermute x2, waiting for transfers between devices, shifted(): return lax.ppermute(x, AXES, pairs)  1.03 us
  transfers between devices with their start and end apart: 10, of which 5 were waited for; matrix products, arithmetic and copies ran while one was open for 0% of the time, Pallas kernels for 18%

profile of v3, /device:TPU:97, one launch (start us, length us, event | category | flops | bytes accessed | tf_op | source)
XLA Modules:
  0.0 34.7 jit_solution(17530842806526690909)
XLA Ops:
  0.6 0.0 copy-start
  0.6 1.3 %collective-permute-start.4 = (bf16[128,1024]{1,0:T(8,128)(2,1)}, bf16[128,1024]{1,0:T(8,128)(2,1)S(1)}, u32[]{:S(2)}, u32[]{:S(2)}) collective-permute-start(bf16[128,1024]{1,0:T(8,128)(2,1)} %own_hbm.1), channel_id=1, source_target_pairs={{0,2},{1,3},{2,4},{3,5},{4,6},{5,7},{6,8},{7,9},{8,10},{9,11},{10,... | collective-permute-start | bytes 786440 | tf_op jit(solution)/shard_map/ppermute | solution.py:190
  1.9 4.3 %collective-permute-start.5 = (bf16[128,1024]{1,0:T(8,128)(2,1)}, bf16[128,1024]{1,0:T(8,128)(2,1)S(1)}, u32[]{:S(2)}, u32[]{:S(2)}) collective-permute-start(bf16[128,1024]{1,0:T(8,128)(2,1)} %own_hbm.1), channel_id=1, source_target_pairs={{0,4},{1,5},{2,6},{3,7},{4,8},{5,9},{6,10},{7,11},{8,12},{9,13},{1... | collective-permute-start | bytes 786440 | tf_op jit(solution)/shard_map/ppermute | solution.py:193
  6.3 1.3 %collective-permute-start.3 = (bf16[128,1024]{1,0:T(8,128)(2,1)}, bf16[128,1024]{1,0:T(8,128)(2,1)S(1)}, u32[]{:S(2)}, u32[]{:S(2)}) collective-permute-start(bf16[128,1024]{1,0:T(8,128)(2,1)} %own_hbm.1), channel_id=1, source_target_pairs={{0,1},{1,0},{2,3},{3,2},{4,5},{5,4},{6,7},{7,6},{8,9},{9,8},{10,11... | collective-permute-start | bytes 786440 | tf_op jit(solution)/shard_map/ppermute | solution.py:196
  7.6 3.4 %collective-permute-start.2 = (bf16[128,1024]{1,0:T(8,128)(2,1)}, bf16[128,1024]{1,0:T(8,128)(2,1)S(1)}, u32[]{:S(2)}, u32[]{:S(2)}) collective-permute-start(bf16[128,1024]{1,0:T(8,128)(2,1)} %refs_0_.1), channel_id=1, source_target_pairs={{0,4},{1,5},{2,6},{3,7},{4,8},{5,9},{6,10},{7,11},{8,12},{9,13},{1... | collective-permute-start | bytes 786440 | tf_op jit(solution)/shard_map/ppermute | solution.py:193
  11.0 1.3 %collective-permute-start.7 = (bf16[128,1024]{1,0:T(8,128)(2,1)}, bf16[128,1024]{1,0:T(8,128)(2,1)S(1)}, u32[]{:S(2)}, u32[]{:S(2)}) collective-permute-start(bf16[128,1024]{1,0:T(8,128)(2,1)} %refs_0_.1), channel_id=1, source_target_pairs={{0,2},{1,3},{2,4},{3,5},{4,6},{5,7},{6,8},{7,9},{8,10},{9,11},{10,... | collective-permute-start | bytes 786440 | tf_op jit(solution)/shard_map/ppermute | solution.py:190
  13.0 0.1 pad_add_fusion.here_ref
  13.0 0.0 collective-permute-done.4.two
  13.0 5.2 %collective-permute-done.5.four = bf16[128,1024]{1,0:T(8,128)(2,1)S(1)} collective-permute-done((bf16[128,1024]{1,0:T(8,128)(2,1)}, bf16[128,1024]{1,0:T(8,128)(2,1)S(1)}, u32[]{:S(2)}, u32[]{:S(2)}) %collective-permute-start.5) | collective-permute-done | bytes 262176 | tf_op jit(solution)/shard_map/ppermute | solution.py:193
  18.2 4.5 %conditional.1 = (bf16[128,1024]{1,0:T(8,128)(2,1)}, bf16[128,1024]{1,0:T(8,128)(2,1)}) conditional(s32[]{:T(128)} %bitcast.3, (bf16[128,1024]{1,0:T(8,128)(2,1)S(1)}, bf16[128,1024]{1,0:T(8,128)(2,1)S(1)}) %tuple.17, (bf16[128,1024]{1,0:T(8,128)(2,1)S(1)}, bf16[128,1024]{1,0:T(8,128)(2,1)S(1)}) %tuple.17), branch_computations={%region_0.1_spmd, %region_1.2_spmd} | conditional | bytes 2097248 | solution.py:202
  18.2 2.8 %collective-permute-start = (bf16[128,1024]{1,0:T(8,128)(2,1)S(1)}, bf16[128,1024]{1,0:T(8,128)(2,1)}, u32[]{:S(2)}, u32[]{:S(2)}) collective-permute-start(bf16[128,1024]{1,0:T(8,128)(2,1)S(1)} %get-tuple-element.8), channel_id=1, source_target_pairs={{0,1},{1,0},{2,3},{3,2},{4,5},{5,4},{6,7},{7,6},{8,9},{9,8},{10,11... | collective-permute-start | bytes 786440 | tf_op jit(solution)/shard_map/cond/branch_1_fun/ppermute | solution.py:196
  21.0 0.0 collective-permute-start.1
  21.0 1.3 %collective-permute-done = bf16[128,1024]{1,0:T(8,128)(2,1)} collective-permute-done((bf16[128,1024]{1,0:T(8,128)(2,1)S(1)}, bf16[128,1024]{1,0:T(8,128)(2,1)}, u32[]{:S(2)}, u32[]{:S(2)}) %collective-permute-start) | collective-permute-done | bytes 262176 | tf_op jit(solution)/shard_map/cond/branch_1_fun/ppermute | solution.py:196
  22.3 0.4 %collective-permute-done.1 = bf16[128,1024]{1,0:T(8,128)(2,1)} collective-permute-done((bf16[128,1024]{1,0:T(8,128)(2,1)S(1)}, bf16[128,1024]{1,0:T(8,128)(2,1)}, u32[]{:S(2)}, u32[]{:S(2)}) %collective-permute-start.1) | collective-permute-done | bytes 262176 | tf_op jit(solution)/shard_map/cond/branch_1_fun/ppermute | solution.py:196
  22.7 0.0 collective-permute-done.3.near
  22.7 6.2 %scores.1 = (bf16[4096,512]{1,0:T(8,128)(2,1)S(1)}, f32[32,128]{1,0:T(8,128)S(1)}, f32[32,128]{1,0:T(8,128)}) custom-call(s32[2]{0:T(128)S(1)} %pad_add_fusion.here_ref, bf16[128,1024]{1,0:T(8,128)(2,1)S(1)} %collective-permute-done.3.near, bf16[128,1024]{1,0:T(8,128)(2,1)S(1)} %collective-permute-done.4.two, ...), custom_call_target="tpu_custom_call" | custom-call | flops 671088640 | bytes 8388608 | tf_op jit(solution)/shard_map/scores/pallas_call | solution.py:131
  28.9 0.0 collective-permute-done.2.refs_4_
  28.9 0.4 %collective-permute-start.8 = (bf16[128,1024]{1,0:T(8,128)(2,1)S(1)}, bf16[128,1024]{1,0:T(8,128)(2,1)S(1)}, u32[]{:S(2)}, u32[]{:S(2)}) collective-permute-start(bf16[128,1024]{1,0:T(8,128)(2,1)S(1)} %collective-permute-done.2.refs_4_), channel_id=1, source_target_pairs={{0,1},{1,0},{2,3},{3,2},{4,5},{5,4},{6,7},{7,6},{8,9},{9,8},{10,11... | collective-permute-start | bytes 786440 | tf_op jit(solution)/shard_map/ppermute | solution.py:196
  29.3 0.0 copy-done
  29.3 0.1 collective-permute-start.6
  29.5 1.0 %collective-permute-done.7.refs_2_ = bf16[128,1024]{1,0:T(8,128)(2,1)S(1)} collective-permute-done((bf16[128,1024]{1,0:T(8,128)(2,1)}, bf16[128,1024]{1,0:T(8,128)(2,1)S(1)}, u32[]{:S(2)}, u32[]{:S(2)}) %collective-permute-start.7) | collective-permute-done | bytes 262176 | tf_op jit(solution)/shard_map/ppermute | solution.py:190
  30.5 0.0 collective-permute-done.8.refs_5_
  30.5 0.5 %collective-permute-start.9 = (bf16[128,1024]{1,0:T(8,128)(2,1)S(1)}, bf16[128,1024]{1,0:T(8,128)(2,1)S(1)}, u32[]{:S(2)}, u32[]{:S(2)}) collective-permute-start(bf16[128,1024]{1,0:T(8,128)(2,1)S(1)} %collective-permute-done.7.refs_2_), channel_id=1, source_target_pairs={{0,1},{1,0},{2,3},{3,2},{4,5},{5,4},{6,7},{7,6},{8,9},{9,8},{10,11... | collective-permute-start | bytes 786440 | tf_op jit(solution)/shard_map/ppermute | solution.py:196
  31.0 0.0 collective-permute-done.6.refs_1_
  31.0 1.2 %collective-permute-done.9.refs_3_ = bf16[128,1024]{1,0:T(8,128)(2,1)S(1)} collective-permute-done((bf16[128,1024]{1,0:T(8,128)(2,1)S(1)}, bf16[128,1024]{1,0:T(8,128)(2,1)S(1)}, u32[]{:S(2)}, u32[]{:S(2)}) %collective-permute-start.9) | collective-permute-done | bytes 262176 | tf_op jit(solution)/shard_map/ppermute | solution.py:196
  32.1 2.6 %values.1 = bf16[128,4096]{1,0:T(8,128)(2,1)} custom-call(s32[2]{0:T(128)S(1)} %pad_add_fusion.here_ref, bf16[4096,512]{1,0:T(8,128)(2,1)S(1)} %get-tuple-element.24.weight_ref, f32[32,128]{1,0:T(8,128)S(1)} %get-tuple-element.25.inverse_ref, bf16[128,1024]{1,0:T(8,128)(2,1)S(1)} %copy-done, bf16[128,1024]{1,0:T(8,128)(2,1)S(1)} %collective-permute-done.6.refs_1_, ...), custom_call_target="tpu_custom_call" | custom-call | flops 671088640 | bytes 8388608 | tf_op jit(solution)/shard_map/values/pallas_call | solution.py:163
Async XLA Ops:
  0.6 28.7 %copy-start = (bf16[128,1024]{1,0:T(8,128)(2,1)S(1)}, bf16[128,1024]{1,0:T(8,128)(2,1)}, u32[]{:S(2)}) copy-start(bf16[128,1024]{1,0:T(8,128)(2,1)} %refs_0_.1) | copy-start | bytes 786436
  0.6 12.4 %collective-permute-start.4 = (bf16[128,1024]{1,0:T(8,128)(2,1)}, bf16[128,1024]{1,0:T(8,128)(2,1)S(1)}, u32[]{:S(2)}, u32[]{:S(2)}) collective-permute-start(bf16[128,1024]{1,0:T(8,128)(2,1)} %own_hbm.1), channel_id=1, source_target_pairs={{0,2},{1,3},{2,4},{3,5},{4,6},{5,7},{6,8},{7,9},{8,10},{9,11},{10,... | collective-permute-start | bytes 786440 | tf_op jit(solution)/shard_map/ppermute | solution.py:190
  1.9 16.3 %collective-permute-start.5 = (bf16[128,1024]{1,0:T(8,128)(2,1)}, bf16[128,1024]{1,0:T(8,128)(2,1)S(1)}, u32[]{:S(2)}, u32[]{:S(2)}) collective-permute-start(bf16[128,1024]{1,0:T(8,128)(2,1)} %own_hbm.1), channel_id=1, source_target_pairs={{0,4},{1,5},{2,6},{3,7},{4,8},{5,9},{6,10},{7,11},{8,12},{9,13},{1... | collective-permute-start | bytes 786440 | tf_op jit(solution)/shard_map/ppermute | solution.py:193
  6.3 16.4 %collective-permute-start.3 = (bf16[128,1024]{1,0:T(8,128)(2,1)}, bf16[128,1024]{1,0:T(8,128)(2,1)S(1)}, u32[]{:S(2)}, u32[]{:S(2)}) collective-permute-start(bf16[128,1024]{1,0:T(8,128)(2,1)} %own_hbm.1), channel_id=1, source_target_pairs={{0,1},{1,0},{2,3},{3,2},{4,5},{5,4},{6,7},{7,6},{8,9},{9,8},{10,11... | collective-permute-start | bytes 786440 | tf_op jit(solution)/shard_map/ppermute | solution.py:196
  7.6 21.3 %collective-permute-start.2 = (bf16[128,1024]{1,0:T(8,128)(2,1)}, bf16[128,1024]{1,0:T(8,128)(2,1)S(1)}, u32[]{:S(2)}, u32[]{:S(2)}) collective-permute-start(bf16[128,1024]{1,0:T(8,128)(2,1)} %refs_0_.1), channel_id=1, source_target_pairs={{0,4},{1,5},{2,6},{3,7},{4,8},{5,9},{6,10},{7,11},{8,12},{9,13},{1... | collective-permute-start | bytes 786440 | tf_op jit(solution)/shard_map/ppermute | solution.py:193
  11.0 19.5 %collective-permute-start.7 = (bf16[128,1024]{1,0:T(8,128)(2,1)}, bf16[128,1024]{1,0:T(8,128)(2,1)S(1)}, u32[]{:S(2)}, u32[]{:S(2)}) collective-permute-start(bf16[128,1024]{1,0:T(8,128)(2,1)} %refs_0_.1), channel_id=1, source_target_pairs={{0,2},{1,3},{2,4},{3,5},{4,6},{5,7},{6,8},{7,9},{8,10},{9,11},{10,... | collective-permute-start | bytes 786440 | tf_op jit(solution)/shard_map/ppermute | solution.py:190
  18.2 4.1 %collective-permute-start = (bf16[128,1024]{1,0:T(8,128)(2,1)S(1)}, bf16[128,1024]{1,0:T(8,128)(2,1)}, u32[]{:S(2)}, u32[]{:S(2)}) collective-permute-start(bf16[128,1024]{1,0:T(8,128)(2,1)S(1)} %get-tuple-element.8), channel_id=1, source_target_pairs={{0,1},{1,0},{2,3},{3,2},{4,5},{5,4},{6,7},{7,6},{8,9},{9,8},{10,11... | collective-permute-start | bytes 786440 | tf_op jit(solution)/shard_map/cond/branch_1_fun/ppermute | solution.py:196
  21.0 1.7 %collective-permute-start.1 = (bf16[128,1024]{1,0:T(8,128)(2,1)S(1)}, bf16[128,1024]{1,0:T(8,128)(2,1)}, u32[]{:S(2)}, u32[]{:S(2)}) collective-permute-start(bf16[128,1024]{1,0:T(8,128)(2,1)S(1)} %get-tuple-element.9), channel_id=1, source_target_pairs={{0,1},{1,0},{2,3},{3,2},{4,5},{5,4},{6,7},{7,6},{8,9},{9,8},{10,11... | collective-permute-start | bytes 786440 | tf_op jit(solution)/shard_map/cond/branch_1_fun/ppermute | solution.py:196
  28.9 1.6 %collective-permute-start.8 = (bf16[128,1024]{1,0:T(8,128)(2,1)S(1)}, bf16[128,1024]{1,0:T(8,128)(2,1)S(1)}, u32[]{:S(2)}, u32[]{:S(2)}) collective-permute-start(bf16[128,1024]{1,0:T(8,128)(2,1)S(1)} %collective-permute-done.2.refs_4_), channel_id=1, source_target_pairs={{0,1},{1,0},{2,3},{3,2},{4,5},{5,4},{6,7},{7,6},{8,9},{9,8},{10,11... | collective-permute-start | bytes 786440 | tf_op jit(solution)/shard_map/ppermute | solution.py:196
  29.3 1.6 %collective-permute-start.6 = (bf16[128,1024]{1,0:T(8,128)(2,1)S(1)}, bf16[128,1024]{1,0:T(8,128)(2,1)S(1)}, u32[]{:S(2)}, u32[]{:S(2)}) collective-permute-start(bf16[128,1024]{1,0:T(8,128)(2,1)S(1)} %copy-done), channel_id=1, source_target_pairs={{0,1},{1,0},{2,3},{3,2},{4,5},{5,4},{6,7},{7,6},{8,9},{9,8},{10,11... | collective-permute-start | bytes 786440 | tf_op jit(solution)/shard_map/ppermute | solution.py:196
  30.5 1.6 %collective-permute-start.9 = (bf16[128,1024]{1,0:T(8,128)(2,1)S(1)}, bf16[128,1024]{1,0:T(8,128)(2,1)S(1)}, u32[]{:S(2)}, u32[]{:S(2)}) collective-permute-start(bf16[128,1024]{1,0:T(8,128)(2,1)S(1)} %collective-permute-done.7.refs_2_), channel_id=1, source_target_pairs={{0,1},{1,0},{2,3},{3,2},{4,5},{5,4},{6,7},{7,6},{8,9},{9,8},{10,11... | collective-permute-start | bytes 786440 | tf_op jit(solution)/shard_map/ppermute | solution.py:196
